TPU v7x, 256 devices: a whole 4x4x8 slice. The times are simulated.
256 devices in a mesh: dp: 4 (over x), depth: 2 (over y_hi), tensor: 32 (over y_lo, z, core).
Axes of the slice: x: 4, y: 4 (y_hi: 2, y_lo: 2; y = y_hi * 2 + y_lo), z: 8, core: 2. Of those that a mesh axis runs over, the one named last changes fastest.
Arguments:
- text: bfloat16 [512, 8192], P(('dp', 'tensor')), may hold values from -6 to 6
- vision: bfloat16 [1024, 8192], P(('dp', 'depth'), 'tensor'), may hold values from -6 to 6
- query_weight: bfloat16 [2, 8192, 8192], P('depth', None, 'tensor'), may hold values from -0.0625 to 0.0625
- key_weight: bfloat16 [2, 8192, 1024], P('depth', 'tensor'), may hold values from -0.0625 to 0.0625
- value_weight: bfloat16 [2, 8192, 1024], P('depth', 'tensor'), may hold values from -0.0625 to 0.0625
- out_weight: bfloat16 [2, 8192, 8192], P('depth', 'tensor'), may hold values from -0.25 to 0.25
- gate: float32 [2], P('depth'), may hold values from 0.5 to 1.5
- cotangent: bfloat16 [512, 8192], P(('dp', 'tensor')), may hold values from -0.75 to 0.75
- tile_table: int32 [4, 8, 4], P('dp'), may hold values 0 or 1
- vision_tiles: int32 [4], P('dp'), may hold values from 1 to 4
- text_lengths: int32 [4], P('dp'), may hold values from 64 to 128
Outputs:
- hidden_states: bfloat16 [2, 512, 8192], P('depth', ('dp', 'tensor'))
- text_grads: bfloat16 [2, 512, 8192], P('depth', ('dp', 'tensor'))
- vision_grad: float32 [1024, 8192], P(('dp', 'depth'), 'tensor')
- key_weight_grad: float32 [2, 8192, 1024], P('depth', 'tensor', 'dp')
- value_weight_grad: float32 [2, 8192, 1024], P('depth', 'tensor', 'dp')
All inputs are finite; a program needn't handle non-finite values. No bound on the sum of `tile_table` on one device may be relied on, other than what follows from the above.
Results may differ from a plain program's by a relative error of at most 0.034.
Values may be sent and summed in bfloat16 or wider, within the bound.
No kernel may reach another device: no remote copies, remote signals or barrier semaphores. Data moves between devices by JAX's collectives and lax.ppermute only.
A program may use at most 128 MiB of HBM per device.

v0:
```python
import math

import jax
import jax.numpy as jnp
from jax import lax
from jax.sharding import PartitionSpec as P

HD = 128
QGROUP = 8
SEQ = 128
TBLK = 16
TILES = 4
TILE_ROWS = 64
VIS = 256


def shifted(value, axis, steps):
    count = lax.axis_size(axis)
    first, last = (max(0, -steps), min(count, count - steps))
    return lax.ppermute(value, axis, [(source, source + steps) for source in range(first, last)])


def normalize(values, epsilon):
    return values * lax.rsqrt(jnp.mean(values * values, axis=-1, keepdims=True) + epsilon)


def norm_back(values, upstream, epsilon):
    inv_rms = lax.rsqrt(jnp.mean(values * values, axis=-1, keepdims=True) + epsilon)
    normed = values * inv_rms
    return inv_rms * (upstream - normed * jnp.mean(upstream * normed, axis=-1, keepdims=True))


def allowed_mask(table, tile_count, text_count):
    tile_ok = jnp.arange(TILES, dtype=jnp.int32) < tile_count
    block_ok = (table > 0) & tile_ok[None, :]
    full_mask = jnp.broadcast_to(
        block_ok[:, None, :, None], (SEQ // TBLK, TBLK, TILES, TILE_ROWS)
    ).reshape(SEQ, VIS)
    row_ok = jnp.arange(SEQ, dtype=jnp.int32) < text_count
    return full_mask & row_ok[:, None]


def token_rows(shard, transform):
    return transform(lax.all_gather(shard, "tensor", axis=0, tiled=True), jnp.int32(0))


def token_sums(term, shard_rows):
    return lax.psum_scatter(
        term(jnp.int32(0), shard_rows * lax.axis_size("tensor")).astype(jnp.bfloat16),
        "tensor",
        scatter_dimension=0,
        tiled=True,
    ).astype(jnp.float32)


def kv_totals(keys_part, values_part):
    return lax.psum((keys_part, values_part), "tensor")


def per_device(
    text,
    vision,
    query_weight,
    key_weight,
    value_weight,
    out_weight,
    gate,
    cotangent,
    tile_table,
    vision_tiles,
    text_lengths,
):
    layers = lax.axis_size("depth")
    section_index = lax.axis_index("depth")
    tensor_index = lax.axis_index("tensor")
    w_query = query_weight[0]
    w_key = key_weight[0]
    w_value = value_weight[0]
    w_out = out_weight[0]
    gate_value = jnp.tanh(gate[0])
    local_width = w_query.shape[1]
    local_heads = local_width // HD
    kv_width = w_key.shape[1]
    kv_heads = kv_width // HD
    shard_rows = text.shape[0]
    inv_sqrt = 1.0 / math.sqrt(HD)
    kv_group = tensor_index * local_heads // QGROUP
    allowed = allowed_mask(tile_table[0], vision_tiles[0], text_lengths[0])
    row_live = jnp.any(allowed, axis=-1).astype(jnp.float32)
    vis_full = lax.all_gather(vision, "depth", axis=0, tiled=True)
    keys_part = jnp.dot(vis_full, w_key, preferred_element_type=jnp.float32)
    values_part = jnp.dot(vis_full, w_value, preferred_element_type=jnp.float32)
    keys_pre, values_pre = kv_totals(keys_part, values_part)
    keys_cast = (
        normalize(keys_pre.reshape(VIS, kv_heads, HD), 1e-06)
        .astype(jnp.bfloat16)
        .reshape(VIS, kv_width)
    )
    values_cast = values_pre.astype(jnp.bfloat16)
    key_group = lax.dynamic_slice_in_dim(keys_cast, kv_group * HD, HD, 1)
    value_group = lax.dynamic_slice_in_dim(values_cast, kv_group * HD, HD, 1)
    current = text
    for layer_at in range(layers):

        def project(rows_in, offset):
            normed = normalize(rows_in.astype(jnp.float32), 1e-05).astype(jnp.bfloat16)
            return jnp.dot(normed, w_query, preferred_element_type=jnp.float32)

        layer_queries = token_rows(current, project).reshape(SEQ, local_heads, HD)
        layer_query_cast = normalize(layer_queries, 1e-06).astype(jnp.bfloat16)
        scores = (
            jnp.einsum(
                "shd,vd->hsv", layer_query_cast, key_group, preferred_element_type=jnp.float32
            )
            * inv_sqrt
        )
        expd = jnp.where(allowed[None], jnp.exp(scores), 0.0)
        layer_probs = expd / (
            jnp.sum(expd, axis=-1, keepdims=True) + (1.0 - row_live)[None, :, None]
        )
        layer_probs_cast = layer_probs.astype(jnp.bfloat16)
        mixed = jnp.einsum(
            "hsv,vd->shd", layer_probs_cast, value_group, preferred_element_type=jnp.float32
        )
        mixed_cast = mixed.astype(jnp.bfloat16).reshape(SEQ, local_width)

        def out_term(offset, number):
            return jnp.dot(mixed_cast, w_out, preferred_element_type=jnp.float32)

        attended = token_sums(out_term, shard_rows)
        outputs = (current.astype(jnp.float32) + gate_value * attended).astype(jnp.bfloat16)
        outputs, kept = (outputs, (layer_queries, layer_query_cast, layer_probs, layer_probs_cast))
        chosen = section_index == layer_at
        if layer_at == 0:
            saved_in, saved_out, saved_kept = (current, outputs, kept)
        else:
            saved_in = jnp.where(chosen, current, saved_in)
            saved_out = jnp.where(chosen, outputs, saved_out)
            saved_kept = jax.tree.map(
                lambda fresh, older: jnp.where(chosen, fresh, older), kept, saved_kept
            )
        if layer_at + 1 < layers:
            current = shifted(outputs, "depth", 1)
    upstream = cotangent
    for layer_at in reversed(range(layers)):
        queries, query_cast, probs, probs_cast = saved_kept
        scaled = (gate_value * upstream.astype(jnp.float32)).astype(jnp.bfloat16)

        def back_project(rows_in, offset):
            return jnp.einsum("sd,kd->sk", rows_in, w_out, preferred_element_type=jnp.float32)

        dmixed = token_rows(scaled, back_project).astype(jnp.bfloat16).reshape(SEQ, local_heads, HD)
        dprobs = jnp.einsum("shd,vd->hsv", dmixed, value_group, preferred_element_type=jnp.float32)
        layer_dvalues = jnp.einsum(
            "hsv,shd->vd", probs_cast, dmixed, preferred_element_type=jnp.float32
        )
        dscores = (
            probs * (dprobs - jnp.sum(probs * dprobs, axis=-1, keepdims=True)) * inv_sqrt
        ).astype(jnp.bfloat16)
        dquery_hat = jnp.einsum(
            "hsv,vd->shd", dscores, key_group, preferred_element_type=jnp.float32
        )
        layer_dkeys_hat = jnp.einsum(
            "hsv,shd->vd", dscores, query_cast, preferred_element_type=jnp.float32
        )
        dquery = (
            norm_back(queries, dquery_hat, 1e-06).astype(jnp.bfloat16).reshape(SEQ, local_width)
        )

        def in_term(offset, number):
            return jnp.einsum("sk,dk->sd", dquery, w_query, preferred_element_type=jnp.float32)

        dnormed = token_sums(in_term, shard_rows)
        dinputs = (
            upstream.astype(jnp.float32) + norm_back(saved_in.astype(jnp.float32), dnormed, 1e-05)
        ).astype(jnp.bfloat16)
        dinputs, kv_grads = (dinputs, (layer_dkeys_hat, layer_dvalues))
        chosen = section_index == layer_at
        if layer_at == layers - 1:
            saved_grad, saved_kv = (dinputs, kv_grads)
        else:
            saved_grad = jnp.where(chosen, dinputs, saved_grad)
            saved_kv = jax.tree.map(
                lambda fresh, older: jnp.where(chosen, fresh, older), kv_grads, saved_kv
            )
        if layer_at > 0:
            upstream = shifted(dinputs, "depth", -1)
    dkeys_hat, dvalues = saved_kv
    one_hot = (jnp.arange(kv_heads, dtype=jnp.int32) == kv_group).astype(jnp.float32)
    dkeys_full = (dkeys_hat[:, None, :] * one_hot[None, :, None]).reshape(VIS, kv_width)
    dvalues_full = (dvalues[:, None, :] * one_hot[None, :, None]).reshape(VIS, kv_width)
    dkeys_total, dvalues_total = kv_totals(dkeys_full, dvalues_full)
    dkeys_cast = (
        norm_back(
            keys_pre.reshape(VIS, kv_heads, HD), dkeys_total.reshape(VIS, kv_heads, HD), 1e-06
        )
        .astype(jnp.bfloat16)
        .reshape(VIS, kv_width)
    )
    dvalues_cast = dvalues_total.astype(jnp.bfloat16)
    dvision_part = jnp.einsum(
        "vc,dc->vd", dkeys_cast, w_key, preferred_element_type=jnp.float32
    ) + jnp.einsum("vc,dc->vd", dvalues_cast, w_value, preferred_element_type=jnp.float32)
    dvision = lax.psum_scatter(dvision_part, "depth", scatter_dimension=0, tiled=True)
    dkey_part = jnp.einsum("vd,vc->dc", vis_full, dkeys_cast, preferred_element_type=jnp.float32)
    dvalue_part = jnp.einsum(
        "vd,vc->dc", vis_full, dvalues_cast, preferred_element_type=jnp.float32
    )
    dkey_grad, dvalue_grad = (
        lax.psum_scatter(dkey_part, "dp", scatter_dimension=1, tiled=True),
        lax.psum_scatter(dvalue_part, "dp", scatter_dimension=1, tiled=True),
    )
    return (saved_out[None], saved_grad[None], dvision, dkey_grad[None], dvalue_grad[None])


def solution(mesh):
    in_specs = (
        P(("dp", "tensor"), None),
        P(("dp", "depth"), "tensor"),
        P("depth", None, "tensor"),
        P("depth", "tensor", None),
        P("depth", "tensor", None),
        P("depth", "tensor", None),
        P("depth"),
        P(("dp", "tensor"), None),
        P("dp", None, None),
        P("dp"),
        P("dp"),
    )
    out_specs = (
        P("depth", ("dp", "tensor"), None),
        P("depth", ("dp", "tensor"), None),
        P(("dp", "depth"), "tensor"),
        P("depth", "tensor", "dp"),
        P("depth", "tensor", "dp"),
    )
    return jax.shard_map(
        per_device, mesh=mesh, in_specs=in_specs, out_specs=out_specs, check_vma=False
    )
```

profile of v0, /device:TPU:1, one launch (start us, length us, event | category | flops | bytes accessed | tf_op | source)
XLA Modules:
  0.0 1562.4 jit_solution(4551209075161023634)
XLA Ops:
  7.2 6.5 all_gather.15
  15.8 6.5 copy.96
  24.4 2.5 and_reduce_fusion
  27.3 118.3 %all-reduce.22 = bf16[256,1024]{1,0:T(8,128)(2,1)} all-reduce(f32[256,1024]{1,0:T(8,128)S(1)} %fusion.54), channel_id=1, replica_groups=mesh['dp'=4,'depth'=2,'tensor'=32] {'tensor'}, use_global_device_ids=true, to_apply=%region_0.1 | all-reduce | flops 262144 | bytes 1572864 | tf_op jit(solution)/shard_map/psum | solution.py:57
  145.6 98.3 %all-reduce.13.cloned.1.call-done = f32[256,1024]{1,0:T(8,128)} async-done(((f32[256,1024]{1,0:T(8,128)}), f32[256,1024]{1,0:T(8,128)}) %all-reduce.13.cloned.1.call-update) | async-done | bytes 1048592 | tf_op jit(solution)/shard_map/psum | solution.py:57
  243.9 1.5 copy.99
  248.2 61.3 %all-gather.9.cloned.1.call-done = bf16[32,4,8192]{2,1,0:T(4,128)(2,1)} async-done(((bf16[1,4,8192]{2,1,0:T(4,128)(2,1)}), bf16[32,4,8192]{2,1,0:T(4,128)(2,1)}) %all-gather.9.cloned.1.call-update) | async-done | bytes 2097168 | tf_op jit(solution)/shard_map/all_gather | solution.py:44
  309.5 4.3 reshape.252
  313.8 2.7 multiply_reduce_fusion.1
  317.3 3.7 multiply_reduce_fusion.10
  323.3 2.1 convolution_convert_fusion.3
  328.2 224.7 %all-reduce.17.cloned.1.call-done = bf16[128,8192]{1,0:T(8,128)(2,1)} async-done(((bf16[128,8192]{1,0:T(8,128)(2,1)}), bf16[128,8192]{1,0:T(8,128)(2,1)}) %all-reduce.17.cloned.1.call-update) | async-done | bytes 2097168
  553.9 4.3 collective-permute-start
  560.5 58.4 %all-gather.13.cloned.1.call-done = bf16[32,4,8192]{2,1,0:T(4,128)(2,1)} async-done(((bf16[1,4,8192]{2,1,0:T(4,128)(2,1)}), bf16[32,4,8192]{2,1,0:T(4,128)(2,1)}) %all-gather.13.cloned.1.call-update) | async-done | bytes 2097168 | tf_op jit(solution)/shard_map/all_gather | solution.py:44
  618.8 4.0 reshape.249
  622.8 4.4 fusion.43
  627.1 1.7 convolution_bitcast_fusion.3
  628.9 56.7 %all-gather.11.cloned.1.call-done = bf16[32,4,8192]{2,1,0:T(4,128)(2,1)} async-done(((bf16[1,4,8192]{2,1,0:T(4,128)(2,1)}), bf16[32,4,8192]{2,1,0:T(4,128)(2,1)}) %all-gather.11.cloned.1.call-update) | async-done | bytes 2097168 | tf_op jit(solution)/shard_map/all_gather | solution.py:44
  685.5 4.3 reshape.253
  689.9 2.7 multiply_reduce_fusion
  693.3 3.6 multiply_reduce_fusion.9
  698.9 1.5 multiply_reduce_fusion.7
  700.5 5.1 convolution_convert_fusion.1
  705.9 226.9 %all-reduce.19.cloned.1.call-done = bf16[128,8192]{1,0:T(8,128)(2,1)} async-done(((bf16[128,8192]{1,0:T(8,128)(2,1)}), bf16[128,8192]{1,0:T(8,128)(2,1)}) %all-reduce.19.cloned.1.call-update) | async-done | bytes 2097168
  936.3 5.2 collective-permute-done.1
  942.4 2.1 convolution_bitcast_fusion.6
  945.3 59.2 %all-gather.15.cloned.1.call-done = bf16[32,4,8192]{2,1,0:T(4,128)(2,1)} async-done(((bf16[1,4,8192]{2,1,0:T(4,128)(2,1)}), bf16[32,4,8192]{2,1,0:T(4,128)(2,1)}) %all-gather.15.cloned.1.call-update) | async-done | bytes 2097168 | tf_op jit(solution)/shard_map/all_gather | solution.py:44
  1004.5 4.0 reshape.251
  1008.5 4.4 fusion.40
  1012.9 1.7 convolution_bitcast_fusion.2
  1014.8 1.5 fusion.38
  1016.4 1.8 bitcast_multiply_fusion
  1018.3 113.1 %all-reduce.23 = bf16[256,1024]{1,0:T(8,128)(2,1)S(1)} all-reduce(f32[256,1024]{1,0:T(8,128)} %get-tuple-element.29), channel_id=1, replica_groups=mesh['dp'=4,'depth'=2,'tensor'=32] {'tensor'}, use_global_device_ids=true, to_apply=%region_24.25 | all-reduce | flops 262144 | bytes 1572864 | tf_op jit(solution)/shard_map/psum | solution.py:57
  1131.4 1.3 convolution_bitcast_fusion
  1132.8 109.7 %all-reduce.15.cloned.1.call-done = f32[256,1024]{1,0:T(8,128)} async-done(((f32[256,1024]{1,0:T(8,128)}), f32[256,1024]{1,0:T(8,128)}) %all-reduce.15.cloned.1.call-update) | async-done | bytes 1048592 | tf_op jit(solution)/shard_map/psum | solution.py:57
  1242.5 1.6 copy.102
  1244.1 1.5 multiply_reduce_fusion.2
  1246.8 1.3 convolution_bitcast_fusion.1
  1249.4 4.3 convolution_convert_fusion.2
  1253.7 1.5 multiply_reduce_fusion.6
  1255.3 5.0 convolution_convert_fusion
  1262.4 5.8 reduce-scatter.8.cloned.1.call-done
  1268.3 1.8 copy.79
  1270.0 26.7 %reduce-scatter.6.cloned.1.call-done = f32[256,256]{0,1:T(8,128)} async-done(((f32[256,1024]{0,1:T(8,128)}), f32[256,256]{0,1:T(8,128)}) %reduce-scatter.6.cloned.1.call-update) | async-done | bytes 262160 | tf_op jit(solution)/shard_map/reduce_scatter | solution.py:210
  1296.7 1.8 copy.78
  1298.5 237.2 %all-reduce.21.cloned.1.call-done = (bf16[128,8192]{1,0:T(8,128)(2,1)}, bf16[128,8192]{1,0:T(8,128)(2,1)}) async-done(((bf16[128,8192]{1,0:T(8,128)(2,1)}, bf16[128,8192]{1,0:T(8,128)(2,1)}), (bf16[128,8192]{1,0:T(8,128)(2,1)}, bf16[128,8192]{1,0:T(8,128)(2,1)})) %all-reduce.21.cloned.1.call-update) | async-done | bytes 4194320
  1536.9 1.8 fusion.84
  1538.8 16.8 %reduce-scatter.4.cloned.1.call-done = f32[128,256]{1,0:T(8,128)} async-done(((f32[256,256]{1,0:T(8,128)}), f32[128,256]{1,0:T(8,128)}) %reduce-scatter.4.cloned.1.call-update) | async-done | bytes 131088 | tf_op jit(solution)/shard_map/reduce_scatter | solution.py:204
  (146 shorter events, 27.7 us)
Async XLA Ops:
  7.2 6.5 copy-start
  7.2 236.7 %all-reduce.13.cloned.1.call-start = ((), (), s32[]{:S(2)}) async-start(), calls=%async_computation.3 | async-start | bytes 2097152 | tf_op jit(solution)/shard_map/psum | solution.py:57
  15.0 294.5 %all-gather.9.cloned.1.call-start = ((), (), s32[]{:S(2)}) async-start(), calls=%async_computation.8 | async-start | bytes 2162688 | tf_op jit(solution)/shard_map/all_gather | solution.py:44
  15.8 537.2 %all-reduce.17.cloned.1.call-start = ((), (), s32[]{:S(2)}) async-start(), calls=%async_computation.12 | async-start | bytes 4194304
  15.8 7.2 copy-start.29
  15.8 11.1 copy-start.8
  243.9 3.3 copy-start.4
  245.8 68.0 %copy-start.10 = (f32[256,8]{1,0:T(8,128)}, f32[256,8]{1,0:T(8,128)S(1)}, u32[]{:S(2)}) copy-start(f32[256,8]{1,0:T(8,128)S(1)} %add_rsqrt_fusion) | copy-start | bytes 24580
  246.2 1.0 copy-start.5
  313.8 3.4 copy-start.2
  317.3 6.0 copy-start.1
  321.1 1.1 copy-start.26
  322.1 3.3 copy-start.13
  323.3 2.9 copy-start.24
  323.3 3.6 copy-start.30
  323.3 229.6 %copy-start.15 = (bf16[4,8192]{1,0:T(4,128)(2,1)S(1)}, bf16[4,8192]{1,0:T(4,128)(2,1)}, u32[]{:S(2)}) copy-start(bf16[4,8192]{1,0:T(4,128)(2,1)} %param.11) | copy-start | bytes 196612
  325.5 293.4 %all-gather.13.cloned.1.call-start = ((), (), s32[]{:S(2)}) async-start(), calls=%async_computation.10 | async-start | bytes 2162688 | tf_op jit(solution)/shard_map/all_gather | solution.py:44
  326.9 358.6 %all-gather.11.cloned.1.call-start = ((), (), s32[]{:S(2)}) async-start(), calls=%async_computation.9 | async-start | bytes 2162688 | tf_op jit(solution)/shard_map/all_gather | solution.py:44
  553.9 143.1 %copy-start.20 = (bf16[4,8192]{1,0:T(4,128)(2,1)}, bf16[4,8192]{1,0:T(4,128)(2,1)S(1)}, u32[]{:S(2)}) copy-start(bf16[4,8192]{1,0:T(4,128)(2,1)S(1)} %add_convert_fusion.1) | copy-start | bytes 196612
  553.9 5.7 collective-permute-start
  559.6 0.6 copy-start.16
  560.2 372.6 %all-reduce.19.cloned.1.call-start = ((), (), s32[]{:S(2)}) async-start(), calls=%async_computation.13 | async-start | bytes 4194304
  689.9 3.4 copy-start.3
  693.3 4.9 copy-start.14
  697.0 3.5 copy-start.28
  697.0 8.6 copy-start.11
  700.5 5.2 copy-start.17
  700.5 233.5 %copy-start.25 = (bf16[4,8192]{1,0:T(4,128)(2,1)S(1)}, bf16[4,8192]{1,0:T(4,128)(2,1)}, u32[]{:S(2)}) copy-start(bf16[4,8192]{1,0:T(4,128)(2,1)} %param.18) | copy-start | bytes 196612
  700.5 241.9 %copy-start.27 = (bf16[128,2,128]{0,2,1:T(8,128)(2,1)S(1)}, bf16[128,2,128]{0,2,1:T(8,128)(2,1)}, u32[]{:S(2)}) copy-start(bf16[128,2,128]{0,2,1:T(8,128)(2,1)} %copy-done.26) | copy-start | bytes 196612
  705.6 298.8 %all-gather.15.cloned.1.call-start = ((), (), s32[]{:S(2)}) async-start(), calls=%async_computation.11 | async-start | bytes 2162688 | tf_op jit(solution)/shard_map/all_gather | solution.py:44
  935.0 77.8 %copy-start.22 = (bf16[4,8192]{1,0:T(4,128)(2,1)}, bf16[4,8192]{1,0:T(4,128)(2,1)S(1)}, u32[]{:S(2)}) copy-start(bf16[4,8192]{1,0:T(4,128)(2,1)S(1)} %fusion.69) | copy-start | bytes 196612
  935.0 6.5 collective-permute-start.1
  942.2 300.3 %all-reduce.15.cloned.1.call-start = ((), (), s32[]{:S(2)}) async-start(), calls=%async_computation.4 | async-start | bytes 2097152 | tf_op jit(solution)/shard_map/psum | solution.py:57
  1008.5 6.1 copy-start.19
  1018.3 250.0 %reduce-scatter.8.cloned.1.call-start = ((), (), s32[]{:S(2)}) async-start(), calls=%async_computation.7 | async-start | bytes 1310720 | tf_op jit(solution)/shard_map/reduce_scatter | solution.py:211
  1132.8 163.9 %reduce-scatter.6.cloned.1.call-start = ((), (), s32[]{:S(2)}) async-start(), calls=%async_computation.6 | async-start | bytes 1310720 | tf_op jit(solution)/shard_map/reduce_scatter | solution.py:210
  1242.5 3.5 copy-start.6
  1242.5 3.5 copy-start.7
  1248.1 5.6 copy-start.12
  1248.1 287.6 %all-reduce.21.cloned.1.call-start = ((), (), s32[]{:S(2)}) async-start(), calls=%async_computation.14 | async-start | bytes 8388608
  1260.3 1.1 copy-start.9
  1260.3 276.6 %copy-start.18 = (bf16[4,8192]{1,0:T(4,128)(2,1)S(1)}, bf16[4,8192]{1,0:T(4,128)(2,1)}, u32[]{:S(2)}) copy-start(bf16[4,8192]{1,0:T(4,128)(2,1)} %copy-done.16) | copy-start | bytes 196612
  1260.3 276.6 %copy-start.21 = (bf16[4,8192]{1,0:T(4,128)(2,1)S(1)}, bf16[4,8192]{1,0:T(4,128)(2,1)}, u32[]{:S(2)}) copy-start(bf16[4,8192]{1,0:T(4,128)(2,1)} %copy-done.20) | copy-start | bytes 196612
  1260.3 276.6 %copy-start.23 = (bf16[4,8192]{1,0:T(4,128)(2,1)S(1)}, bf16[4,8192]{1,0:T(4,128)(2,1)}, u32[]{:S(2)}) copy-start(bf16[4,8192]{1,0:T(4,128)(2,1)} %copy-done.22) | copy-start | bytes 196612
  1260.3 295.2 %reduce-scatter.4.cloned.1.call-start = ((), (), s32[]{:S(2)}) async-start(), calls=%async_computation.5 | async-start | bytes 393216 | tf_op jit(solution)/shard_map/reduce_scatter | solution.py:204
Sparse Core Ops, SparseCore 0:
  15.1 228.7 all-reduce.12
  245.9 63.5 all-gather.8
  325.6 227.2 all-reduce.16
  555.2 63.5 all-gather.12
  621.1 64.3 all-gather.10
  705.8 226.9 all-reduce.18
  942.4 62.0 all-gather.14
  1018.4 224.0 all-reduce.14
  1245.1 23.1 reduce-scatter.7
  1270.8 25.8 reduce-scatter.5
  1299.4 236.2 all-reduce.20
  1538.6 16.8 reduce-scatter.3
where the time goes:
time: 1560 us
  waiting for transfers between devices  1190 us (76%)
  blocking collectives  238 us (15%)
  matrix products  53.6 us (3%)
  local copies, waits for them, and re-layouts  35.6 us (2%)
  other arithmetic  22.3 us (1%)
  between operations  17.5 us (1%)
    unnamed x15, waiting for transfers between devices  690 us
    all_gather x4, waiting for transfers between devices, token_rows(): lax.all_gather(shard, 'tensor', axis=0, tiled=True)  235 us
    psum x2, blocking collectives, kv_totals(): return lax.psum((keys_part, values_part), 'tensor')  231 us
    psum x2, waiting for transfers between devices, kv_totals(): return lax.psum((keys_part, values_part), 'tensor')  208 us
  transfers between devices with their start and end apart: 14, of which 14 were waited for; matrix products, arithmetic and copies ran while one was open for 4% of the time, Pallas kernels for 0%

commit v1 on v0

v1 whole, which is shorter than its diff:
```python
import math

import jax
import jax.numpy as jnp
from jax import lax
from jax.experimental import pallas as pl
from jax.experimental.pallas import tpu as pltpu
from jax.sharding import PartitionSpec as P

HD = 128
SEQ = 128
TBLK = 16
TILES = 4
TILE_ROWS = 64
VIS = 256
NT = 32
INV_SQRT = 1.0 / math.sqrt(HD)
BF = jnp.bfloat16
F32 = jnp.float32


def moved(move):
    pairs = []
    for t in range(NT):
        y, z, c = move(t // 16, (t // 2) % 8, t % 2)
        pairs.append((t, y * 16 + z * 2 + c))
    return pairs


TO_CORE = moved(lambda y, z, c: (y, z, 1 - c))
TO_ROW = moved(lambda y, z, c: (1 - y, z, c))
KV_PAIR = moved(lambda y, z, c: (y, z ^ 1, c))
KV_BOTH = moved(lambda y, z, c: (y, z ^ 1, 1 - c))
CHIPS = NT // 2
CHIP_GROUPS = [[2 * chip + c for chip in range(CHIPS)] for c in range(2)]
RING = 8
RING_GROUPS = [[16 * y + 2 * z + c for z in range(RING)] for y in range(2) for c in range(2)]
ROWS = SEQ // NT
HALF = SEQ // 2


def hop(value, pairs):
    return lax.ppermute(value, "tensor", pairs)


def chip_exchange(value):
    return lax.all_to_all(value, "tensor", 0, 0, axis_index_groups=CHIP_GROUPS)


def ring_exchange(value):
    return lax.all_to_all(value, "tensor", 0, 0, axis_index_groups=RING_GROUPS)


def after(value, earlier):
    return lax.optimization_barrier((value, earlier))[0]


def gather_chips(shard):
    near = chip_exchange(jnp.broadcast_to(shard[None], (CHIPS,) + shard.shape))
    return near, hop(near, TO_CORE)


def normalize(values, epsilon):
    return values * lax.rsqrt(jnp.mean(values * values, axis=-1, keepdims=True) + epsilon)


def norm_back(values, upstream, epsilon):
    inv_rms = lax.rsqrt(jnp.mean(values * values, axis=-1, keepdims=True) + epsilon)
    normed = values * inv_rms
    return inv_rms * (upstream - normed * jnp.mean(upstream * normed, axis=-1, keepdims=True))


def dot_nt(a, b):
    return lax.dot_general(a, b, (((1,), (1,)), ((), ())), preferred_element_type=F32)


def dot_tn(a, b):
    return lax.dot_general(a, b, (((0,), (0,)), ((), ())), preferred_element_type=F32)


def dot_nn(a, b):
    return lax.dot_general(a, b, (((1,), (0,)), ((), ())), preferred_element_type=F32)


def head_probs(query, keys, allowed):
    query_cast = normalize(query, 1e-06).astype(BF)
    scores = dot_nt(query_cast, keys) * INV_SQRT
    expd = jnp.where(allowed > 0.0, jnp.exp(scores), 0.0)
    live = jnp.max(allowed, axis=-1, keepdims=True)
    probs = expd / (jnp.sum(expd, axis=-1, keepdims=True) + (1.0 - live))
    return query_cast, probs


def local_call(kernel, outs, ins, name, scratch=()):
    held = pl.BlockSpec(memory_space=pltpu.VMEM)
    return pl.pallas_call(
        kernel,
        in_specs=[held] * len(ins),
        out_specs=[held] * len(outs),
        out_shape=[jax.ShapeDtypeStruct(shape, dtype) for shape, dtype in outs],
        scratch_shapes=list(scratch),
        compiler_params=pltpu.CompilerParams(vmem_limit_bytes=24 * 1024 * 1024),
        name=name,
    )(*ins)


STEP = 1024


def projected(near_ref, far_ref, weight_ref, transposed):
    total = 0.0
    for at in range(0, near_ref.shape[-1], STEP):
        rows = [
            ref[:, :, at : at + STEP].astype(F32).reshape(HALF, STEP) for ref in (near_ref, far_ref)
        ]
        rows = jnp.concatenate(rows, axis=0).astype(BF)
        if transposed:
            total += dot_nt(rows, weight_ref[:, at : at + STEP])
        else:
            total += dot_nn(rows, weight_ref[at : at + STEP, :])
    return total


def mix(query_ref, keys, values, allowed, mixed_ref):
    for at in range(0, query_ref.shape[1], HD):
        _, probs = head_probs(query_ref[:, at : at + HD], keys, allowed)
        mixed_ref[:, at : at + HD] = dot_nn(probs.astype(BF), values).astype(BF)


def mix_back(query_ref, dmixed_ref, keys, values, allowed, dquery_ref, dkv_ref):
    dkeys = 0.0
    dvalues = 0.0
    for at in range(0, query_ref.shape[1], HD):
        query = query_ref[:, at : at + HD]
        query_cast, probs = head_probs(query, keys, allowed)
        dmixed = dmixed_ref[:, at : at + HD].astype(BF)
        dprobs = dot_nt(dmixed, values)
        dvalues += dot_tn(probs.astype(BF), dmixed)
        dscores = (
            probs * (dprobs - jnp.sum(probs * dprobs, axis=-1, keepdims=True)) * INV_SQRT
        ).astype(BF)
        dkeys += dot_tn(dscores, query_cast)
        dquery_ref[:, at : at + HD] = norm_back(query, dot_nn(dscores, keys), 1e-06).astype(BF)
    dkv_ref[:, :HD] = dkeys
    dkv_ref[:, HD:] = dvalues


def project(near, far, weight, transposed):
    def kernel(near_ref, far_ref, weight_ref, sum_ref):
        sum_ref[...] = projected(near_ref, far_ref, weight_ref, transposed)

    width = weight.shape[0] if transposed else weight.shape[1]
    return local_call(kernel, [((SEQ, width), F32)], [near, far, weight], "project")[0]


def attend(query, keys, values, allowed):
    def kernel(query_ref, keys_ref, values_ref, allowed_ref, mixed_ref):
        mix(query_ref, keys_ref[...], values_ref[...], allowed_ref[...], mixed_ref)

    return local_call(kernel, [(query.shape, BF)], [query, keys, values, allowed], "attend")[0]


def query_back(near, far, weight, dmixed, keys, values, allowed):
    def kernel(
        near_ref,
        far_ref,
        weight_ref,
        dmixed_ref,
        keys_ref,
        values_ref,
        allowed_ref,
        query_ref,
        dquery_ref,
        dkv_ref,
    ):
        query_ref[...] = projected(near_ref, far_ref, weight_ref, False)
        kv = (keys_ref[...], values_ref[...])
        mix_back(query_ref, dmixed_ref, *kv, allowed_ref[...], dquery_ref, dkv_ref)

    shape = (SEQ, weight.shape[1])
    return local_call(
        kernel,
        [(shape, F32), (shape, BF), ((VIS, 2 * HD), F32)],
        [near, far, weight, dmixed, keys, values, allowed],
        "query_back",
    )


def dmixed_back(near, far, weight, query, keys, values, allowed):
    def kernel(
        near_ref,
        far_ref,
        weight_ref,
        query_ref,
        keys_ref,
        values_ref,
        allowed_ref,
        dquery_ref,
        dkv_ref,
        dmixed_ref,
    ):
        dmixed_ref[...] = projected(near_ref, far_ref, weight_ref, True)
        kv = (keys_ref[...], values_ref[...])
        mix_back(query_ref, dmixed_ref, *kv, allowed_ref[...], dquery_ref, dkv_ref)

    return local_call(
        kernel,
        [(query.shape, BF), ((VIS, 2 * HD), F32)],
        [near, far, weight, query, keys, values, allowed],
        "dmixed_back",
        [pltpu.VMEM(query.shape, F32)],
    )


def weight_block(weight_ref, at, transposed):
    return weight_ref[at : at + STEP, :] if transposed else weight_ref[:, at : at + STEP]


def product(rows, weight, transposed):
    width = weight.shape[0] if transposed else weight.shape[1]

    def kernel(rows_ref, weight_ref, out_ref):
        dot = dot_nt if transposed else dot_nn
        for at in range(0, width, STEP):
            block = weight_block(weight_ref, at, transposed)
            out_ref[:, at : at + STEP] = dot(rows_ref[...], block).astype(BF)

    return local_call(kernel, [((HALF, width), BF)], [rows, weight], "product")[0]


def product_sum(rows, weight, arrived, transposed):
    width = arrived.shape[1]

    def kernel(rows_ref, weight_ref, arrived_ref, out_ref):
        dot = dot_nt if transposed else dot_nn
        for at in range(0, width, STEP):
            total = dot(rows_ref[...], weight_block(weight_ref, at, transposed))
            total += arrived_ref[:, at : at + STEP].astype(F32)
            out_ref[:, :, at : at + STEP] = total.reshape(CHIPS, ROWS, STEP).astype(BF)

    return local_call(
        kernel, [((CHIPS, ROWS, width), BF)], [rows, weight, arrived], "product_sum"
    )[0]


def chosen_product(first, rows, in_weight, out_weight):
    width = out_weight.shape[1]

    def kernel(first_ref, rows_ref, in_ref, out_weight_ref, out_ref):
        for transposed, ref in ((True, in_ref), (False, out_weight_ref)):

            @pl.when(first_ref[0] == int(transposed))
            def _():
                dot = dot_nt if transposed else dot_nn
                for at in range(0, width, STEP):
                    block = weight_block(ref, at, transposed)
                    out_ref[:, at : at + STEP] = dot(rows_ref[...], block).astype(BF)

    return chosen_call(
        kernel, ((HALF, width), BF), first, [rows, in_weight, out_weight], "chosen_product"
    )


def chosen_product_sum(first, rows, in_weight, out_weight, arrived):
    width = out_weight.shape[1]

    def kernel(first_ref, rows_ref, in_ref, out_weight_ref, arrived_ref, out_ref):
        for transposed, ref in ((True, in_ref), (False, out_weight_ref)):

            @pl.when(first_ref[0] == int(transposed))
            def _():
                dot = dot_nt if transposed else dot_nn
                for at in range(0, width, STEP):
                    total = dot(rows_ref[...], weight_block(ref, at, transposed))
                    total += arrived_ref[:, at : at + STEP].astype(F32)
                    out_ref[:, :, at : at + STEP] = total.reshape(CHIPS, ROWS, STEP).astype(BF)

    return chosen_call(
        kernel,
        ((CHIPS, ROWS, width), BF),
        first,
        [rows, in_weight, out_weight, arrived],
        "chosen_product_sum",
    )


def chosen_call(kernel, out, first, ins, name):
    held = pl.BlockSpec(memory_space=pltpu.VMEM)
    return pl.pallas_call(
        kernel,
        in_specs=[pl.BlockSpec(memory_space=pltpu.SMEM)] + [held] * len(ins),
        out_specs=held,
        out_shape=jax.ShapeDtypeStruct(*out),
        compiler_params=pltpu.CompilerParams(vmem_limit_bytes=24 * 1024 * 1024),
        name=name,
    )(first.astype(jnp.int32).reshape(1), *ins)


def token_sums(away_product, near_product, rows):
    away = away_product(rows[HALF:])
    return near_product(rows[:HALF], hop(away, TO_CORE))


def token_totals(terms):
    return jnp.sum(chip_exchange(terms).astype(F32), axis=0)


def kv_product(rows, w_key, w_value, arrived=None):
    def kernel(rows_ref, key_ref, value_ref, *refs):
        out_ref = refs[-1]
        for which, ref in enumerate((key_ref, value_ref)):
            part = dot_nn(rows_ref[...], ref[...])
            lanes = slice(which * HD, which * HD + HD)
            for chip in range(CHIPS):
                head, half = chip // 2, chip % 2
                piece = part[
                    half * TILE_ROWS : (half + 1) * TILE_ROWS, head * HD : (head + 1) * HD
                ]
                if arrived is not None:
                    piece = piece + refs[0][chip, :, lanes].astype(F32)
                out_ref[chip, :, lanes] = piece.astype(BF)

    more = [] if arrived is None else [arrived]
    return local_call(
        kernel,
        [((CHIPS, TILE_ROWS, 2 * HD), BF)],
        [rows, w_key, w_value, *more],
        "kv_product",
    )[0]


def vision_back(near, far, w_key, w_value):
    def kernel(near_ref, far_ref, key_ref, value_ref, out_ref):
        for core, ref in enumerate((near_ref, far_ref)):
            for half in range(2):
                total = 0.0
                for head in range(CHIPS // 2):
                    lanes = slice(head * HD, head * HD + HD)
                    piece = ref[2 * head + half]
                    total += dot_nt(piece[:, :HD], key_ref[:, lanes])
                    total += dot_nt(piece[:, HD:], value_ref[:, lanes])
                out_ref[half, core] = total

    return local_call(
        kernel,
        [((2, 2, TILE_ROWS, w_key.shape[0]), F32)],
        [near, far, w_key, w_value],
        "vision_back",
    )[0]


def weight_back(visions, near, far):
    samples = len(visions)
    heads = near.shape[0] // samples // 2

    def kernel(*refs):
        vision_refs = refs[:samples]
        near_ref, far_ref, key_ref, value_ref = refs[samples:]
        vision = jnp.concatenate([ref[...] for ref in vision_refs], axis=0)
        for head in range(heads):
            pieces = [
                ref[(sample * heads + head) * 2 + half]
                for sample in range(samples)
                for ref in (near_ref, far_ref)
                for half in range(2)
            ]
            total = dot_tn(vision, jnp.concatenate(pieces, axis=0))
            lanes = slice(head * HD, head * HD + HD)
            key_ref[:, lanes] = total[:, :HD]
            value_ref[:, lanes] = total[:, HD:]

    shape = ((visions[0].shape[-1], heads * HD), F32)
    return local_call(kernel, [shape, shape], [*visions, near, far], "weight_back")


def per_device(
    text,
    vision,
    query_weight,
    key_weight,
    value_weight,
    out_weight,
    gate,
    cotangent,
    tile_table,
    vision_tiles,
    text_lengths,
):
    section = lax.axis_index("depth")
    first = section == 0
    tensor = lax.axis_index("tensor")
    core = tensor % 2
    row = tensor // 16
    tile = tensor % 4
    w_key = key_weight[0]
    w_value = value_weight[0]
    gate_value = jnp.tanh(gate[0])
    depth_swap = [(0, 1), (1, 0)]
    text_f = text.astype(F32)
    cotangent_f = cotangent.astype(F32)

    opening = jnp.where(first, normalize(text_f, 1e-05), gate_value * cotangent_f).astype(BF)
    w_query = query_weight[0]
    w_out = out_weight[0]
    opened_near = chip_exchange(jnp.broadcast_to(opening[None], (CHIPS,) + opening.shape))

    place = jnp.arange(SEQ, dtype=jnp.int32)
    side = jnp.bitwise_xor(core, place // HALF)
    row_at = (place % HALF) // ROWS * (2 * ROWS) + side * ROWS + place % ROWS
    tile_ok = jnp.arange(TILES, dtype=jnp.int32) < vision_tiles[0]
    block_ok = ((tile_table[0] > 0) & tile_ok[None, :]).astype(BF)
    in_block = (row_at // TBLK)[:, None] == jnp.arange(SEQ // TBLK, dtype=jnp.int32)[None, :]
    in_block = in_block & (row_at < text_lengths[0])[:, None]
    column_tile = jnp.bitwise_xor(tile, jnp.arange(VIS, dtype=jnp.int32) // TILE_ROWS)
    in_tile = jnp.arange(TILES, dtype=jnp.int32)[:, None] == column_tile[None, :]
    allowed = dot_nn(dot_nn(in_block.astype(BF), block_ok).astype(BF), in_tile.astype(BF))

    other = lax.ppermute(vision, "depth", depth_swap)
    tiles = vision.reshape(2, TILE_ROWS, vision.shape[1])
    other_tiles = other.reshape(2, TILE_ROWS, vision.shape[1])

    def tiles_of(which):
        mine = jnp.where(which == 0, tiles[0], tiles[1])
        theirs = jnp.where(which == 0, other_tiles[0], other_tiles[1])
        return jnp.concatenate(
            [jnp.where(first, mine, theirs), jnp.where(first, theirs, mine)], axis=0
        )

    vision_near = tiles_of(core)
    vision_far = tiles_of(1 - core)
    vision_pair = jnp.concatenate([vision_near, vision_far], axis=0)
    samples = lax.axis_size("dp")

    def sample_hop(value, step):
        pairs = [(at, (at + step) % samples) for at in range(samples)]
        return lax.ppermute(value, "dp", pairs)

    vision_all = [vision_pair] + [sample_hop(vision_pair, step) for step in range(1, samples)]
    arrived = hop(kv_product(vision_far, w_key, w_value), TO_CORE)
    pieces = kv_product(vision_near, w_key, w_value, arrived)
    opened_near, pieces, vision_all = lax.optimization_barrier((opened_near, pieces, vision_all))
    opened = (opened_near, hop(opened_near, TO_CORE))
    query_first = project(*opened, w_query, False)
    pieces = after(chip_exchange(pieces), query_first)
    piece = jnp.sum(pieces.astype(F32), axis=0)
    keys_piece = piece[:, :HD]
    kv_piece = jnp.concatenate([normalize(keys_piece, 1e-06), piece[:, HD:]], axis=1).astype(BF)
    head_kv = jnp.concatenate(
        [kv_piece, hop(kv_piece, TO_CORE), hop(kv_piece, KV_PAIR), hop(kv_piece, KV_BOTH)], axis=0
    )
    keys = head_kv[:, :HD]
    values = head_kv[:, HD:]

    def out_sums(rows):
        return token_sums(
            lambda part: product(part, w_out, False),
            lambda part, arrived: product_sum(part, w_out, arrived, False),
            rows,
        )

    def in_sums(rows):
        return token_sums(
            lambda part: product(part, w_query, True),
            lambda part, arrived: product_sum(part, w_query, arrived, True),
            rows,
        )

    def last_sums(rows):
        return token_sums(
            lambda part: chosen_product(first, part, w_query, w_out),
            lambda part, arrived: chosen_product_sum(first, part, w_query, w_out, arrived),
            rows,
        )

    dmixed_second = project(*opened, w_out, True)
    mixed_first = attend(query_first, keys, values, allowed)
    hidden_first = (text_f + gate_value * token_totals(out_sums(mixed_first))).astype(BF)

    passed = lax.ppermute(hidden_first, "depth", [(0, 1)])
    passed_f = passed.astype(F32)
    middle = gather_chips(normalize(passed_f, 1e-05).astype(BF))
    query_second, dquery_second, dkv_second = query_back(
        *middle, w_query, dmixed_second, keys, values, allowed
    )
    dnormed = token_totals(in_sums(dquery_second))
    grad_second = (cotangent_f + norm_back(passed_f, dnormed, 1e-05)).astype(BF)
    mixed_second = attend(query_second, keys, values, allowed)

    upstream = lax.ppermute(grad_second, "depth", [(1, 0)])
    upstream_f = upstream.astype(F32)
    closing = gather_chips((gate_value * upstream_f).astype(BF))
    dquery_first, dkv_first = dmixed_back(*closing, w_out, query_first, keys, values, allowed)

    dkv = jnp.where(first, dkv_first, dkv_second)
    dkv_piece = (
        dkv[:TILE_ROWS]
        + hop(dkv[TILE_ROWS : 2 * TILE_ROWS], TO_CORE)
        + hop(dkv[2 * TILE_ROWS : 3 * TILE_ROWS], KV_PAIR)
        + hop(dkv[3 * TILE_ROWS :], KV_BOTH)
    )
    dkv_piece = jnp.concatenate(
        [norm_back(keys_piece, dkv_piece[:, :HD], 1e-06), dkv_piece[:, HD:]], axis=1
    ).astype(BF)
    ring_pieces = ring_exchange(jnp.broadcast_to(dkv_piece[None], (RING,) + dkv_piece.shape))
    last_terms = last_sums(jnp.where(first, dquery_first, mixed_second))
    ring_pieces, last_terms = lax.optimization_barrier((ring_pieces, last_terms))
    other_pieces = hop(ring_pieces, TO_ROW)
    pieces_near = jnp.concatenate(
        [
            jnp.where(row == 0, ring_pieces, other_pieces),
            jnp.where(row == 0, other_pieces, ring_pieces),
        ],
        axis=0,
    )
    pieces_far = hop(pieces_near, TO_CORE)
    sample = lax.axis_index("dp")
    share = CHIPS // samples
    columns = []
    for step in range(samples):
        start = (sample + step) % samples * share
        column = lax.dynamic_slice_in_dim(pieces_near, start, share, 0)
        columns.append(sample_hop(column, step) if step else column)
    columns_near = jnp.concatenate(columns, axis=0)
    columns_far = hop(columns_near, TO_CORE)
    key_grad, value_grad = weight_back(vision_all, columns_near, columns_far)
    dvision = vision_back(pieces_near, pieces_far, w_key, w_value)
    mine = lax.dynamic_index_in_dim(dvision, section, 0, False)
    theirs = lax.dynamic_index_in_dim(dvision, 1 - section, 0, False)
    dvision = mine + lax.ppermute(theirs, "depth", depth_swap)
    dvision = jnp.where(core == 0, dvision, dvision[::-1]).reshape(VIS // 2, vision.shape[1])

    last = token_totals(last_terms)
    grad_first = (upstream_f + norm_back(text_f, last, 1e-05)).astype(BF)
    hidden_second = (passed_f + gate_value * last).astype(BF)
    hidden = jnp.where(first, hidden_first, hidden_second)
    text_grad = jnp.where(first, grad_first, grad_second)
    return (hidden[None], text_grad[None], dvision, key_grad[None], value_grad[None])


def solution(mesh):
    in_specs = (
        P(("dp", "tensor"), None),
        P(("dp", "depth"), "tensor"),
        P("depth", None, "tensor"),
        P("depth", "tensor", None),
        P("depth", "tensor", None),
        P("depth", "tensor", None),
        P("depth"),
        P(("dp", "tensor"), None),
        P("dp", None, None),
        P("dp"),
        P("dp"),
    )
    out_specs = (
        P("depth", ("dp", "tensor"), None),
        P("depth", ("dp", "tensor"), None),
        P(("dp", "depth"), "tensor"),
        P("depth", "tensor", "dp"),
        P("depth", "tensor", "dp"),
    )
    return jax.shard_map(
        per_device, mesh=mesh, in_specs=in_specs, out_specs=out_specs, check_vma=False
    )
```

time: 1560 us -> 295 us (0.19)
  waiting for transfers between devices: 1190 us -> 45.6 us
  blocking collectives: 238 us -> 120 us
  starting transfers between devices: 6.54 us -> 68.6 us
  matrix products: 53.6 us -> 1 us
  Pallas kernels: 0 us -> 21.3 us
    unnamed x15 -> x0, waiting for transfers between devices: 690 us -> none
    all_gather x4 -> x0, waiting for transfers between devices: 235 us -> none  [token_rows(): lax.all_gather(shard, 'tensor', axis=0, tiled=True)]
    psum x2 -> x0, blocking collectives: 231 us -> none  [kv_totals(): return lax.psum((keys_part, values_part), 'tensor')]
    psum x2 -> x0, waiting for transfers between devices: 208 us -> none  [kv_totals(): return lax.psum((keys_part, values_part), 'tensor')]
    all_to_all x0 -> x4, blocking collectives: none -> 120 us  [chip_exchange(): return lax.all_to_all(value, 'tensor', 0, 0, axis_index_groups=CHIP_GROUPS)]
    dot_general x26 -> x1, matrix products: 53.6 us -> 1 us  [dot_nn(): lax.dot_general(a, b, (((1,), (0,)), ((), ())), preferred_element_type=F32)]
    reduce_scatter x3 -> x0, waiting for transfers between devices: 49.3 us -> none  [the longest x1 26.7 us: per_device(): lax.psum_scatter(dkey_part, 'dp', scatter_dimension=1, tiled=True)]
    ppermute x2 -> x26, starting transfers between devices: 5.64 us -> 45.4 us  [the longest x16 28.3 us: hop(): return lax.ppermute(value, 'tensor', pairs)]
  transfers between devices with their start and end apart: 14 -> 30, of which waited for: 14 -> 17; matrix products, arithmetic and copies ran while one was open for 4% -> 2% of each run, Pallas kernels for 0% -> 3%
where the time goes in v1:
time: 295 us; the launch traced here: 293 us
  blocking collectives  120 us (41%)
  starting transfers between devices  68.6 us (23%)
  waiting for transfers between devices  45.6 us (15%)
  Pallas kernels  21.3 us (7%)
  local copies, waits for them, and re-layouts  20.2 us (7%)
  other arithmetic  12.3 us (4%)
  between operations  3.47 us (1%)
    all_to_all x4, blocking collectives, chip_exchange(): return lax.all_to_all(value, 'tensor', 0, 0, axis_index_groups=CHIP_GROUPS)  120 us
    ppermute x16, starting transfers between devices, hop(): return lax.ppermute(value, 'tensor', pairs)  28.3 us
    all_to_all x3, starting transfers between devices, chip_exchange(): return lax.all_to_all(value, 'tensor', 0, 0, axis_index_groups=CHIP_GROUPS)  18.7 us
    pallas_call x14, Pallas kernels, local_call(): pl.pallas_call(kernel, in_specs=[held] * len(ins), out_specs=[held] * len...  17.6 us
    unnamed x70, local copies, waits for them, and re-layouts  17.2 us
    all_to_all x3, waiting for transfers between devices, chip_exchange(): return lax.all_to_all(value, 'tensor', 0, 0, axis_index_groups=CHIP_GROUPS)  12.7 us
    ppermute x16, waiting for transfers between devices, hop(): return lax.ppermute(value, 'tensor', pairs)  9.39 us
    ppermute x6, starting transfers between devices, sample_hop(): return lax.ppermute(value, 'dp', pairs)  8.58 us
  transfers between devices with their start and end apart: 30, of which 17 were waited for; matrix products, arithmetic and copies ran while one was open for 2% of the time, Pallas kernels for 3%

profile of v1, /device:TPU:1, one launch (start us, length us, event | category | flops | bytes accessed | tf_op | source)
XLA Modules:
  0.0 292.5 jit_solution(357960521344173473)
XLA Ops:
  3.5 1.4 broadcast_in_dim.16
  4.9 10.1 %all-to-all-start = ((bf16[16,4,8192]{2,1,0:T(4,128)(2,1)}), bf16[16,4,8192]{2,1,0:T(4,128)(2,1)S(1)}, u32[]{:S(2)}, u32[]{:S(2)}) async-start(bf16[16,4,8192]{2,1,0:T(4,128)(2,1)} %broadcast_in_dim.16), calls=%async_computation | async-start | bytes 2097152 | tf_op jit(solution)/shard_map/all_to_all | solution.py:47
  15.0 2.7 collective-permute-start
  17.7 2.6 collective-permute-done
  20.7 2.9 %collective-permute-start.1 = (bf16[16,64,256]{2,1,0:T(8,128)(2,1)S(1)}, bf16[16,64,256]{2,1,0:T(8,128)(2,1)S(1)}, u32[]{:S(2)}, u32[]{:S(2)}) collective-permute-start(bf16[16,64,256]{2,1,0:T(8,128)(2,1)S(1)} %kv_product.2), channel_id=1, source_target_pairs={{0,1},{1,0},{2,3},{3,2},{4,5},{5,4},{6,7},{7,6},{8,9},{9,8},{10,11... | collective-permute-start | bytes 1572872 | tf_op jit(solution)/shard_map/ppermute | solution.py:43
  23.7 2.5 collective-permute-start.4
  28.5 3.3 %collective-permute-done.4.refs_3_ = bf16[256,256]{1,0:T(8,128)(2,1)S(1)} collective-permute-done((bf16[256,256]{1,0:T(8,128)(2,1)S(1)}, bf16[256,256]{1,0:T(8,128)(2,1)S(1)}, u32[]{:S(2)}, u32[]{:S(2)}) %collective-permute-start.4) | collective-permute-done | bytes 131104 | tf_op jit(solution)/shard_map/ppermute | solution.py:436
  33.2 2.7 collective-permute-done.2.refs_1_
  36.6 4.1 %all-to-all-done.near_ref = bf16[16,4,8192]{2,1,0:T(4,128)(2,1)S(1)} async-done(((bf16[16,4,8192]{2,1,0:T(4,128)(2,1)}), bf16[16,4,8192]{2,1,0:T(4,128)(2,1)S(1)}, u32[]{:S(2)}, u32[]{:S(2)}) %all-to-all-start) | async-done | bytes 1048608 | tf_op jit(solution)/shard_map/all_to_all | solution.py:47
  40.7 2.3 collective-permute-start.5
  43.0 4.2 %all-to-all-start.1 = ((bf16[16,64,256]{2,1,0:T(8,128)(2,1)}), bf16[16,64,256]{2,1,0:T(8,128)(2,1)}, u32[]{:S(2)}, u32[]{:S(2)}) async-start(bf16[16,64,256]{2,1,0:T(8,128)(2,1)} %copy-done.10), calls=%async_computation.1 | async-start | bytes 1048576 | tf_op jit(solution)/shard_map/all_to_all | solution.py:47
  50.1 2.2 copy-done
  53.1 8.7 %all-to-all-done.1 = bf16[16,64,256]{2,1,0:T(8,128)(2,1)} async-done(((bf16[16,64,256]{2,1,0:T(8,128)(2,1)}), bf16[16,64,256]{2,1,0:T(8,128)(2,1)}, u32[]{:S(2)}, u32[]{:S(2)}) %all-to-all-start.1) | async-done | bytes 524320 | tf_op jit(solution)/shard_map/all_to_all | solution.py:47
  63.1 3.5 %collective-permute-start.8 = (bf16[64,256]{1,0:T(8,128)(2,1)S(1)}, bf16[64,256]{1,0:T(8,128)(2,1)S(1)}, u32[]{:S(2)}, u32[]{:S(2)}) collective-permute-start(bf16[64,256]{1,0:T(8,128)(2,1)S(1)} %pad_maximum_fusion.6), channel_id=1, source_target_pairs={{0,3},{1,2},{2,1},{3,0},{4,7},{5,6},{6,5},{7,4},{8,11},{9,10},{10,... | collective-permute-start | bytes 98312 | tf_op jit(solution)/shard_map/ppermute | solution.py:43
  70.8 2.2 copy-done.4
  74.1 2.5 collective-permute-done.9.arrived_ref
  77.6 29.3 %all_to_all.40 = bf16[16,4,8192]{2,1,0:T(4,128)(2,1)S(1)} all-to-all(bf16[16,4,8192]{2,1,0:T(4,128)(2,1)S(1)} %product_sum.2), channel_id=1, replica_groups={{0,2,4,6,8,10,12,14,16,18,20,22,24,26,28,30},{1,3,5,7,9,11,13,15,17,19,..., dimensions={0} | all-to-all | bytes 2097152 | tf_op jit(solution)/shard_map/all_to_all | solution.py:47
  107.4 4.2 %collective-permute-start.10 = (bf16[4,8192]{1,0:T(4,128)(2,1)S(1)}, bf16[4,8192]{1,0:T(4,128)(2,1)S(1)}, u32[]{:S(2)}, u32[]{:S(2)}) collective-permute-start(bf16[4,8192]{1,0:T(4,128)(2,1)S(1)} %fusion.18), channel_id=1, source_target_pairs={{0,32},{1,33},{2,34},{3,35},{4,36},{5,37},{6,38},{7,39},{8,40},{9,... | collective-permute-start | bytes 196616 | tf_op jit(solution)/shard_map/ppermute | solution.py:479
  111.7 1.3 collective-permute-done.10
  113.7 30.5 %all_to_all.41.near_ref = bf16[16,4,8192]{2,1,0:T(4,128)(2,1)S(1)} all-to-all(bf16[16,4,8192]{2,1,0:T(4,128)(2,1)S(1)} %broadcast_in_dim.17), channel_id=1, replica_groups={{0,2,4,6,8,10,12,14,16,18,20,22,24,26,28,30},{1,3,5,7,9,11,13,15,17,19,..., dimensions={0} | all-to-all | bytes 2097152 | tf_op jit(solution)/shard_map/all_to_all | solution.py:47
  144.2 3.0 %collective-permute-start.11 = (bf16[16,4,8192]{2,1,0:T(4,128)(2,1)S(1)}, bf16[16,4,8192]{2,1,0:T(4,128)(2,1)S(1)}, u32[]{:S(2)}, u32[]{:S(2)}) collective-permute-start(bf16[16,4,8192]{2,1,0:T(4,128)(2,1)S(1)} %all_to_all.41.near_ref), channel_id=1, source_target_pairs={{0,1},{1,0},{2,3},{3,2},{4,5},{5,4},{6,7},{7,6},{8,9},{9,8},{10,11... | collective-permute-start | bytes 3145736 | tf_op jit(solution)/shard_map/ppermute | solution.py:43
  147.2 1.5 project.3.dmixed_ref
  149.5 2.0 query_back.1
  152.2 1.4 product.3
  154.0 2.3 collective-permute-done.12.arrived_ref
  156.3 1.4 product_sum.3
  157.7 29.6 %all_to_all.42 = bf16[16,4,8192]{2,1,0:T(4,128)(2,1)S(1)} all-to-all(bf16[16,4,8192]{2,1,0:T(4,128)(2,1)S(1)} %product_sum.3), channel_id=1, replica_groups={{0,2,4,6,8,10,12,14,16,18,20,22,24,26,28,30},{1,3,5,7,9,11,13,15,17,19,..., dimensions={0} | all-to-all | bytes 2097152 | tf_op jit(solution)/shard_map/all_to_all | solution.py:47
  189.5 5.5 %collective-permute-done.13 = bf16[4,8192]{1,0:T(4,128)(2,1)S(1)} collective-permute-done((bf16[4,8192]{1,0:T(4,128)(2,1)S(1)}, bf16[4,8192]{1,0:T(4,128)(2,1)S(1)}, u32[]{:S(2)}, u32[]{:S(2)}) %collective-permute-start.13) | collective-permute-done | bytes 65568 | tf_op jit(solution)/shard_map/ppermute | solution.py:489
  195.4 30.6 %all_to_all.43.near_ref = bf16[16,4,8192]{2,1,0:T(4,128)(2,1)S(1)} all-to-all(bf16[16,4,8192]{2,1,0:T(4,128)(2,1)S(1)} %broadcast_in_dim.18), channel_id=1, replica_groups={{0,2,4,6,8,10,12,14,16,18,20,22,24,26,28,30},{1,3,5,7,9,11,13,15,17,19,..., dimensions={0} | all-to-all | bytes 2097152 | tf_op jit(solution)/shard_map/all_to_all | solution.py:47
  226.0 3.0 %collective-permute-start.14 = (bf16[16,4,8192]{2,1,0:T(4,128)(2,1)S(1)}, bf16[16,4,8192]{2,1,0:T(4,128)(2,1)}, u32[]{:S(2)}, u32[]{:S(2)}) collective-permute-start(bf16[16,4,8192]{2,1,0:T(4,128)(2,1)S(1)} %all_to_all.43.near_ref), channel_id=1, source_target_pairs={{0,1},{1,0},{2,3},{3,2},{4,5},{5,4},{6,7},{7,6},{8,9},{9,8},{10,11... | collective-permute-start | bytes 3145736 | tf_op jit(solution)/shard_map/ppermute | solution.py:43
  229.7 1.7 collective-permute-done.14.far_ref
  231.4 2.2 copy-done.6
  233.6 4.0 %dmixed_back.1 = (bf16[128,256]{1,0:T(8,128)(2,1)S(1)}, f32[256,256]{1,0:T(8,128)S(1)}) custom-call(bf16[16,4,8192]{2,1,0:T(4,128)(2,1)S(1)} %all_to_all.43.near_ref, bf16[16,4,8192]{2,1,0:T(4,128)(2,1)} %collective-permute-done.14.far_ref, bf16[256,8192]{1,0:T(8,128)(2,1)S(1)} %bitcast.34, f32[128,256]{1,0:T(8,128)S(1)} %project.2.query_ref, ...), custom_call_target="tpu_custom_call" | custom-call | tf_op jit(solution)/shard_map/dmixed_back/pallas_call | solution.py:96
  238.1 1.6 collective-permute-start.17
  239.7 1.4 chosen_product.1
  243.9 4.5 %all-to-all-start.6 = ((bf16[8,64,256]{2,1,0:T(8,128)(2,1)}), bf16[8,64,256]{2,1,0:T(8,128)(2,1)S(1)}, u32[]{:S(2)}, u32[]{:S(2)}) async-start(bf16[8,64,256]{2,1,0:T(8,128)(2,1)} %broadcast_in_dim.19), calls=%async_computation.6 | async-start | bytes 524288 | tf_op jit(solution)/shard_map/all_to_all | solution.py:51
  248.4 2.2 copy-done.3
  250.6 2.2 copy-done.7
  252.8 2.4 chosen_product_sum.1
  255.2 3.4 %all-to-all-done.6 = bf16[8,64,256]{2,1,0:T(8,128)(2,1)S(1)} async-done(((bf16[8,64,256]{2,1,0:T(8,128)(2,1)}), bf16[8,64,256]{2,1,0:T(8,128)(2,1)S(1)}, u32[]{:S(2)}, u32[]{:S(2)}) %all-to-all-start.6) | async-done | bytes 262176 | tf_op jit(solution)/shard_map/all_to_all | solution.py:51
  259.5 4.3 %all-to-all-start.7 = ((bf16[16,4,8192]{2,1,0:T(4,128)(2,1)}), bf16[16,4,8192]{2,1,0:T(4,128)(2,1)}, u32[]{:S(2)}, u32[]{:S(2)}) async-start(bf16[16,4,8192]{2,1,0:T(4,128)(2,1)} %chosen_product_sum.1), calls=%async_computation.7 | async-start | bytes 2097152 | tf_op jit(solution)/shard_map/all_to_all | solution.py:47
  265.5 2.4 collective-permute-start.23
  269.2 5.1 %collective-permute-start.20 = (bf16[16,64,256]{2,1,0:T(8,128)(2,1)S(1)}, bf16[16,64,256]{2,1,0:T(8,128)(2,1)S(1)}, u32[]{:S(2)}, u32[]{:S(2)}) collective-permute-start(bf16[16,64,256]{2,1,0:T(8,128)(2,1)S(1)} %pad_maximum_fusion.near_ref), channel_id=1, source_target_pairs={{0,1},{1,0},{2,3},{3,2},{4,5},{5,4},{6,7},{7,6},{8,9},{9,8},{10,11... | collective-permute-start | bytes 1572872 | tf_op jit(solution)/shard_map/ppermute | solution.py:43
  274.4 3.4 %collective-permute-start.25 = (bf16[16,64,256]{2,1,0:T(8,128)(2,1)S(1)}, bf16[16,64,256]{2,1,0:T(8,128)(2,1)S(1)}, u32[]{:S(2)}, u32[]{:S(2)}) collective-permute-start(bf16[16,64,256]{2,1,0:T(8,128)(2,1)S(1)} %pad_maximum_fusion.1.refs_4_), channel_id=1, source_target_pairs={{0,1},{1,0},{2,3},{3,2},{4,5},{5,4},{6,7},{7,6},{8,9},{9,8},{10,11... | collective-permute-start | bytes 1572872 | tf_op jit(solution)/shard_map/ppermute | solution.py:43
  277.9 1.5 vision_back.1
  283.7 4.5 %collective-permute-done.21 = f32[2,64,256]{2,1,0:T(8,128)S(1)} collective-permute-done((f32[2,64,256]{2,1,0:T(8,128)S(1)}, f32[2,64,256]{2,1,0:T(8,128)S(1)}, u32[]{:S(2)}, u32[]{:S(2)}) %collective-permute-start.21) | collective-permute-done | bytes 131104 | tf_op jit(solution)/shard_map/ppermute | solution.py:529
  288.9 1.7 convert_reduce_fusion
  290.8 1.7 fusion.33
  (159 shorter events, 35.2 us)
Async XLA Ops:
  0.6 14.4 %copy-start.33 = (bf16[128,256]{1,0:T(8,128)(2,1)S(1)}, bf16[128,256]{1,0:T(8,128)(2,1)}, u32[]{:S(2)}) copy-start(bf16[128,256]{1,0:T(8,128)(2,1)} %param.12) | copy-start | bytes 196612
  0.6 19.7 %copy-start.9 = (bf16[1,256,1024]{2,1,0:T(8,128)(2,1)S(1)}, bf16[1,256,1024]{2,1,0:T(8,128)(2,1)}, u32[]{:S(2)}) copy-start(bf16[1,256,1024]{2,1,0:T(8,128)(2,1)} %param.15) | copy-start | bytes 1572868
  0.7 19.7 %copy-start.8 = (bf16[1,256,1024]{2,1,0:T(8,128)(2,1)S(1)}, bf16[1,256,1024]{2,1,0:T(8,128)(2,1)}, u32[]{:S(2)}) copy-start(bf16[1,256,1024]{2,1,0:T(8,128)(2,1)} %param.14) | copy-start | bytes 1572868
  4.9 35.8 %all-to-all-start = ((bf16[16,4,8192]{2,1,0:T(4,128)(2,1)}), bf16[16,4,8192]{2,1,0:T(4,128)(2,1)S(1)}, u32[]{:S(2)}, u32[]{:S(2)}) async-start(bf16[16,4,8192]{2,1,0:T(4,128)(2,1)} %broadcast_in_dim.16), calls=%async_computation | async-start | bytes 2097152 | tf_op jit(solution)/shard_map/all_to_all | solution.py:47
  15.0 5.3 %collective-permute-start = (bf16[128,256]{1,0:T(8,128)(2,1)S(1)}, bf16[128,256]{1,0:T(8,128)(2,1)S(1)}, u32[]{:S(2)}, u32[]{:S(2)}) collective-permute-start(bf16[128,256]{1,0:T(8,128)(2,1)S(1)} %copy-done.33), channel_id=1, source_target_pairs={{0,32},{32,0},{1,33},{33,1},{2,34},{34,2},{3,35},{35,3},{4,36},{36... | collective-permute-start | bytes 196616 | tf_op jit(solution)/shard_map/ppermute | solution.py:418
  20.7 6.6 %collective-permute-start.1 = (bf16[16,64,256]{2,1,0:T(8,128)(2,1)S(1)}, bf16[16,64,256]{2,1,0:T(8,128)(2,1)S(1)}, u32[]{:S(2)}, u32[]{:S(2)}) collective-permute-start(bf16[16,64,256]{2,1,0:T(8,128)(2,1)S(1)} %kv_product.2), channel_id=1, source_target_pairs={{0,1},{1,0},{2,3},{3,2},{4,5},{5,4},{6,7},{7,6},{8,9},{9,8},{10,11... | collective-permute-start | bytes 1572872 | tf_op jit(solution)/shard_map/ppermute | solution.py:43
  23.6 8.9 %copy-start.11 = (bf16[256,256]{1,0:T(8,128)(2,1)}, bf16[256,256]{1,0:T(8,128)(2,1)S(1)}, u32[]{:S(2)}) copy-start(bf16[256,256]{1,0:T(8,128)(2,1)S(1)} %pad_maximum_fusion.2.refs_0_) | copy-start | bytes 393220
  23.7 8.1 %collective-permute-start.4 = (bf16[256,256]{1,0:T(8,128)(2,1)S(1)}, bf16[256,256]{1,0:T(8,128)(2,1)S(1)}, u32[]{:S(2)}, u32[]{:S(2)}) collective-permute-start(bf16[256,256]{1,0:T(8,128)(2,1)S(1)} %pad_maximum_fusion.2.refs_0_), channel_id=1, source_target_pairs={{0,192},{64,0},{128,64},{192,128},{1,193},{65,1},{129,65},{193,129... | collective-permute-start | bytes 393224 | tf_op jit(solution)/shard_map/ppermute | solution.py:436
  26.2 6.3 %collective-permute-start.3 = (bf16[256,256]{1,0:T(8,128)(2,1)S(1)}, bf16[256,256]{1,0:T(8,128)(2,1)S(1)}, u32[]{:S(2)}, u32[]{:S(2)}) collective-permute-start(bf16[256,256]{1,0:T(8,128)(2,1)S(1)} %pad_maximum_fusion.2.refs_0_), channel_id=1, source_target_pairs={{0,128},{64,192},{128,0},{192,64},{1,129},{65,193},{129,1},{193,65... | collective-permute-start | bytes 393224 | tf_op jit(solution)/shard_map/ppermute | solution.py:436
  26.7 9.2 %collective-permute-start.2 = (bf16[256,256]{1,0:T(8,128)(2,1)S(1)}, bf16[256,256]{1,0:T(8,128)(2,1)S(1)}, u32[]{:S(2)}, u32[]{:S(2)}) collective-permute-start(bf16[256,256]{1,0:T(8,128)(2,1)S(1)} %pad_maximum_fusion.2.refs_0_), channel_id=1, source_target_pairs={{0,64},{64,128},{128,192},{192,0},{1,65},{65,129},{129,193},{193,1... | collective-permute-start | bytes 393224 | tf_op jit(solution)/shard_map/ppermute | solution.py:436
  40.7 9.4 %collective-permute-start.5 = (bf16[16,4,8192]{2,1,0:T(4,128)(2,1)S(1)}, bf16[16,4,8192]{2,1,0:T(4,128)(2,1)S(1)}, u32[]{:S(2)}, u32[]{:S(2)}) collective-permute-start(bf16[16,4,8192]{2,1,0:T(4,128)(2,1)S(1)} %all-to-all-done.near_ref), channel_id=1, source_target_pairs={{0,1},{1,0},{2,3},{3,2},{4,5},{5,4},{6,7},{7,6},{8,9},{9,8},{10,11... | collective-permute-start | bytes 3145736 | tf_op jit(solution)/shard_map/ppermute | solution.py:43
  43.0 18.7 %all-to-all-start.1 = ((bf16[16,64,256]{2,1,0:T(8,128)(2,1)}), bf16[16,64,256]{2,1,0:T(8,128)(2,1)}, u32[]{:S(2)}, u32[]{:S(2)}) async-start(bf16[16,64,256]{2,1,0:T(8,128)(2,1)} %copy-done.10), calls=%async_computation.1 | async-start | bytes 1048576 | tf_op jit(solution)/shard_map/all_to_all | solution.py:47
  52.3 14.8 %copy-start.34 = (s32[1,8,4]{1,2,0:T(4,128)S(1)}, s32[1,8,4]{1,2,0:T(4,128)}, u32[]{:S(2)}) copy-start(s32[1,8,4]{1,2,0:T(4,128)} %param.19) | copy-start | bytes 388
  63.1 5.1 %collective-permute-start.8 = (bf16[64,256]{1,0:T(8,128)(2,1)S(1)}, bf16[64,256]{1,0:T(8,128)(2,1)S(1)}, u32[]{:S(2)}, u32[]{:S(2)}) collective-permute-start(bf16[64,256]{1,0:T(8,128)(2,1)S(1)} %pad_maximum_fusion.6), channel_id=1, source_target_pairs={{0,3},{1,2},{2,1},{3,0},{4,7},{5,6},{6,5},{7,4},{8,11},{9,10},{10,... | collective-permute-start | bytes 98312 | tf_op jit(solution)/shard_map/ppermute | solution.py:43
  66.6 2.8 collective-permute-start.7
  66.6 2.8 collective-permute-start.6
  73.9 2.7 collective-permute-start.9
  77.6 29.8 %copy-start.23 = (bf16[4,8192]{1,0:T(4,128)(2,1)S(1)}, bf16[4,8192]{1,0:T(4,128)(2,1)}, u32[]{:S(2)}) copy-start(bf16[4,8192]{1,0:T(4,128)(2,1)} %param.11) | copy-start | bytes 196612
  107.4 5.8 %copy-start.32 = (bf16[4,8192]{1,0:T(4,128)(2,1)}, bf16[4,8192]{1,0:T(4,128)(2,1)S(1)}, u32[]{:S(2)}) copy-start(bf16[4,8192]{1,0:T(4,128)(2,1)S(1)} %fusion.18) | copy-start | bytes 196612
  107.4 5.5 %collective-permute-start.10 = (bf16[4,8192]{1,0:T(4,128)(2,1)S(1)}, bf16[4,8192]{1,0:T(4,128)(2,1)S(1)}, u32[]{:S(2)}, u32[]{:S(2)}) collective-permute-start(bf16[4,8192]{1,0:T(4,128)(2,1)S(1)} %fusion.18), channel_id=1, source_target_pairs={{0,32},{1,33},{2,34},{3,35},{4,36},{5,37},{6,38},{7,39},{8,40},{9,... | collective-permute-start | bytes 196616 | tf_op jit(solution)/shard_map/ppermute | solution.py:479
  113.0 75.0 %copy-start.21 = (bf16[4,8192]{1,0:T(4,128)(2,1)}, bf16[4,8192]{1,0:T(4,128)(2,1)S(1)}, u32[]{:S(2)}) copy-start(bf16[4,8192]{1,0:T(4,128)(2,1)S(1)} %collective-permute-done.10) | copy-start | bytes 196612
  144.2 5.3 %copy-start.1 = (bf16[1,8192,256]{2,1,0:T(8,128)(2,1)S(1)}, bf16[1,8192,256]{2,1,0:T(8,128)(2,1)}, u32[]{:S(2)}) copy-start(bf16[1,8192,256]{2,1,0:T(8,128)(2,1)} %param.13) | copy-start | bytes 12582916
  144.2 5.3 %collective-permute-start.11 = (bf16[16,4,8192]{2,1,0:T(4,128)(2,1)S(1)}, bf16[16,4,8192]{2,1,0:T(4,128)(2,1)S(1)}, u32[]{:S(2)}, u32[]{:S(2)}) collective-permute-start(bf16[16,4,8192]{2,1,0:T(4,128)(2,1)S(1)} %all_to_all.41.near_ref), channel_id=1, source_target_pairs={{0,1},{1,0},{2,3},{3,2},{4,5},{5,4},{6,7},{7,6},{8,9},{9,8},{10,11... | collective-permute-start | bytes 3145736 | tf_op jit(solution)/shard_map/ppermute | solution.py:43
  153.6 2.7 collective-permute-start.12
  157.7 30.3 %copy-start.27 = (bf16[4,8192]{1,0:T(4,128)(2,1)S(1)}, bf16[4,8192]{1,0:T(4,128)(2,1)}, u32[]{:S(2)}) copy-start(bf16[4,8192]{1,0:T(4,128)(2,1)} %param.18) | copy-start | bytes 196612
  188.2 41.5 %copy-start.28 = (bf16[4,8192]{1,0:T(4,128)(2,1)}, bf16[4,8192]{1,0:T(4,128)(2,1)S(1)}, u32[]{:S(2)}) copy-start(bf16[4,8192]{1,0:T(4,128)(2,1)S(1)} %fusion.7) | copy-start | bytes 196612
  188.2 6.8 %collective-permute-start.13 = (bf16[4,8192]{1,0:T(4,128)(2,1)S(1)}, bf16[4,8192]{1,0:T(4,128)(2,1)S(1)}, u32[]{:S(2)}, u32[]{:S(2)}) collective-permute-start(bf16[4,8192]{1,0:T(4,128)(2,1)S(1)} %fusion.7), channel_id=1, source_target_pairs={{32,0},{33,1},{34,2},{35,3},{36,4},{37,5},{38,6},{39,7},{40,8},{41... | collective-permute-start | bytes 196616 | tf_op jit(solution)/shard_map/ppermute | solution.py:489
  195.0 34.7 %copy-start.30 = (bf16[4,8192]{1,0:T(4,128)(2,1)}, bf16[4,8192]{1,0:T(4,128)(2,1)S(1)}, u32[]{:S(2)}) copy-start(bf16[4,8192]{1,0:T(4,128)(2,1)S(1)} %collective-permute-done.13) | copy-start | bytes 196612
  226.0 5.4 %collective-permute-start.14 = (bf16[16,4,8192]{2,1,0:T(4,128)(2,1)S(1)}, bf16[16,4,8192]{2,1,0:T(4,128)(2,1)}, u32[]{:S(2)}, u32[]{:S(2)}) collective-permute-start(bf16[16,4,8192]{2,1,0:T(4,128)(2,1)S(1)} %all_to_all.43.near_ref), channel_id=1, source_target_pairs={{0,1},{1,0},{2,3},{3,2},{4,5},{5,4},{6,7},{7,6},{8,9},{9,8},{10,11... | collective-permute-start | bytes 3145736 | tf_op jit(solution)/shard_map/ppermute | solution.py:43
  233.6 6.1 %copy-start.2 = (bf16[1,8192,256]{2,1,0:T(8,128)(2,1)S(1)}, bf16[1,8192,256]{2,1,0:T(8,128)(2,1)}, u32[]{:S(2)}) copy-start(bf16[1,8192,256]{2,1,0:T(8,128)(2,1)} %param.13) | copy-start | bytes 12582916
  237.6 4.3 %collective-permute-start.15 = (f32[64,256]{1,0:T(8,128)S(1)}, f32[64,256]{1,0:T(8,128)S(1)}, u32[]{:S(2)}, u32[]{:S(2)}) collective-permute-start(f32[64,256]{1,0:T(8,128)S(1)} %get-tuple-element.43), channel_id=1, source_target_pairs={{0,1},{1,0},{2,3},{3,2},{4,5},{5,4},{6,7},{7,6},{8,9},{9,8},{10,11... | collective-permute-start | bytes 196616 | tf_op jit(solution)/shard_map/ppermute | solution.py:43
  238.1 3.9 %collective-permute-start.17 = (f32[64,256]{1,0:T(8,128)S(1)}, f32[64,256]{1,0:T(8,128)S(1)}, u32[]{:S(2)}, u32[]{:S(2)}) collective-permute-start(f32[64,256]{1,0:T(8,128)S(1)} %get-tuple-element.44), channel_id=1, source_target_pairs={{0,3},{1,2},{2,1},{3,0},{4,7},{5,6},{6,5},{7,4},{8,11},{9,10},{10,... | collective-permute-start | bytes 196616 | tf_op jit(solution)/shard_map/ppermute | solution.py:43
  239.7 3.1 %collective-permute-start.16 = (f32[64,256]{1,0:T(8,128)S(1)}, f32[64,256]{1,0:T(8,128)S(1)}, u32[]{:S(2)}, u32[]{:S(2)}) collective-permute-start(f32[64,256]{1,0:T(8,128)S(1)} %get-tuple-element.45), channel_id=1, source_target_pairs={{0,2},{1,3},{2,0},{3,1},{4,6},{5,7},{6,4},{7,5},{8,10},{9,11},{10,... | collective-permute-start | bytes 196616 | tf_op jit(solution)/shard_map/ppermute | solution.py:43
  241.1 7.3 %collective-permute-start.18 = (bf16[64,8192]{1,0:T(8,128)(2,1)S(1)}, bf16[64,8192]{1,0:T(8,128)(2,1)S(1)}, u32[]{:S(2)}, u32[]{:S(2)}) collective-permute-start(bf16[64,8192]{1,0:T(8,128)(2,1)S(1)} %chosen_product.1), channel_id=1, source_target_pairs={{0,1},{1,0},{2,3},{3,2},{4,5},{5,4},{6,7},{7,6},{8,9},{9,8},{10,11... | collective-permute-start | bytes 3145736 | tf_op jit(solution)/shard_map/ppermute | solution.py:43
  243.9 14.7 %all-to-all-start.6 = ((bf16[8,64,256]{2,1,0:T(8,128)(2,1)}), bf16[8,64,256]{2,1,0:T(8,128)(2,1)S(1)}, u32[]{:S(2)}, u32[]{:S(2)}) async-start(bf16[8,64,256]{2,1,0:T(8,128)(2,1)} %broadcast_in_dim.19), calls=%async_computation.6 | async-start | bytes 524288 | tf_op jit(solution)/shard_map/all_to_all | solution.py:51
  258.6 5.4 %collective-permute-start.19 = (bf16[8,64,256]{2,1,0:T(8,128)(2,1)S(1)}, bf16[8,64,256]{2,1,0:T(8,128)(2,1)S(1)}, u32[]{:S(2)}, u32[]{:S(2)}) collective-permute-start(bf16[8,64,256]{2,1,0:T(8,128)(2,1)S(1)} %all-to-all-done.6), channel_id=1, source_target_pairs={{0,16},{1,17},{2,18},{3,19},{4,20},{5,21},{6,22},{7,23},{8,24},{9,... | collective-permute-start | bytes 786440 | tf_op jit(solution)/shard_map/ppermute | solution.py:43
  259.5 29.3 %all-to-all-start.7 = ((bf16[16,4,8192]{2,1,0:T(4,128)(2,1)}), bf16[16,4,8192]{2,1,0:T(4,128)(2,1)}, u32[]{:S(2)}, u32[]{:S(2)}) async-start(bf16[16,4,8192]{2,1,0:T(4,128)(2,1)} %chosen_product_sum.1), calls=%async_computation.7 | async-start | bytes 2097152 | tf_op jit(solution)/shard_map/all_to_all | solution.py:47
  264.2 10.1 %collective-permute-start.22 = (bf16[4,64,256]{2,1,0:T(8,128)(2,1)S(1)}, bf16[4,64,256]{2,1,0:T(8,128)(2,1)S(1)}, u32[]{:S(2)}, u32[]{:S(2)}) collective-permute-start(bf16[4,64,256]{2,1,0:T(8,128)(2,1)S(1)} %get-tuple-element.38), channel_id=1, source_target_pairs={{0,64},{64,128},{128,192},{192,0},{1,65},{65,129},{129,193},{193,1... | collective-permute-start | bytes 393224 | tf_op jit(solution)/shard_map/ppermute | solution.py:436
  265.5 8.8 %collective-permute-start.23 = (bf16[4,64,256]{2,1,0:T(8,128)(2,1)S(1)}, bf16[4,64,256]{2,1,0:T(8,128)(2,1)S(1)}, u32[]{:S(2)}, u32[]{:S(2)}) collective-permute-start(bf16[4,64,256]{2,1,0:T(8,128)(2,1)S(1)} %get-tuple-element.39), channel_id=1, source_target_pairs={{0,128},{64,192},{128,0},{192,64},{1,129},{65,193},{129,1},{193,65... | collective-permute-start | bytes 393224 | tf_op jit(solution)/shard_map/ppermute | solution.py:436
  268.0 6.4 %collective-permute-start.24 = (bf16[4,64,256]{2,1,0:T(8,128)(2,1)S(1)}, bf16[4,64,256]{2,1,0:T(8,128)(2,1)S(1)}, u32[]{:S(2)}, u32[]{:S(2)}) collective-permute-start(bf16[4,64,256]{2,1,0:T(8,128)(2,1)S(1)} %get-tuple-element.40), channel_id=1, source_target_pairs={{0,192},{64,0},{128,64},{192,128},{1,193},{65,1},{129,65},{193,129... | collective-permute-start | bytes 393224 | tf_op jit(solution)/shard_map/ppermute | solution.py:436
  269.2 10.5 %copy-start.12 = (bf16[256,256]{1,0:T(8,128)(2,1)S(1)}, bf16[256,256]{1,0:T(8,128)(2,1)}, u32[]{:S(2)}) copy-start(bf16[256,256]{1,0:T(8,128)(2,1)} %copy-done.11) | copy-start | bytes 393220
  269.2 8.7 %collective-permute-start.20 = (bf16[16,64,256]{2,1,0:T(8,128)(2,1)S(1)}, bf16[16,64,256]{2,1,0:T(8,128)(2,1)S(1)}, u32[]{:S(2)}, u32[]{:S(2)}) collective-permute-start(bf16[16,64,256]{2,1,0:T(8,128)(2,1)S(1)} %pad_maximum_fusion.near_ref), channel_id=1, source_target_pairs={{0,1},{1,0},{2,3},{3,2},{4,5},{5,4},{6,7},{7,6},{8,9},{9,8},{10,11... | collective-permute-start | bytes 1572872 | tf_op jit(solution)/shard_map/ppermute | solution.py:43
  274.4 5.3 %collective-permute-start.25 = (bf16[16,64,256]{2,1,0:T(8,128)(2,1)S(1)}, bf16[16,64,256]{2,1,0:T(8,128)(2,1)S(1)}, u32[]{:S(2)}, u32[]{:S(2)}) collective-permute-start(bf16[16,64,256]{2,1,0:T(8,128)(2,1)S(1)} %pad_maximum_fusion.1.refs_4_), channel_id=1, source_target_pairs={{0,1},{1,0},{2,3},{3,2},{4,5},{5,4},{6,7},{7,6},{8,9},{9,8},{10,11... | collective-permute-start | bytes 1572872 | tf_op jit(solution)/shard_map/ppermute | solution.py:43
  279.4 11.2 %copy-start.24 = (bf16[4,8192]{1,0:T(4,128)(2,1)S(1)}, bf16[4,8192]{1,0:T(4,128)(2,1)}, u32[]{:S(2)}) copy-start(bf16[4,8192]{1,0:T(4,128)(2,1)} %param.11) | copy-start | bytes 196612
  279.4 11.4 %copy-start.22 = (bf16[4,8192]{1,0:T(4,128)(2,1)S(1)}, bf16[4,8192]{1,0:T(4,128)(2,1)}, u32[]{:S(2)}) copy-start(bf16[4,8192]{1,0:T(4,128)(2,1)} %copy-done.21) | copy-start | bytes 196612
  279.4 11.4 %copy-start.29 = (bf16[4,8192]{1,0:T(4,128)(2,1)S(1)}, bf16[4,8192]{1,0:T(4,128)(2,1)}, u32[]{:S(2)}) copy-start(bf16[4,8192]{1,0:T(4,128)(2,1)} %copy-done.28) | copy-start | bytes 196612
  279.4 11.4 %copy-start.31 = (bf16[4,8192]{1,0:T(4,128)(2,1)S(1)}, bf16[4,8192]{1,0:T(4,128)(2,1)}, u32[]{:S(2)}) copy-start(bf16[4,8192]{1,0:T(4,128)(2,1)} %copy-done.30) | copy-start | bytes 196612
  279.5 8.7 %collective-permute-start.21 = (f32[2,64,256]{2,1,0:T(8,128)S(1)}, f32[2,64,256]{2,1,0:T(8,128)S(1)}, u32[]{:S(2)}, u32[]{:S(2)}) collective-permute-start(f32[2,64,256]{2,1,0:T(8,128)S(1)} %dynamic-slice_bitcast_fusion), channel_id=1, source_target_pairs={{0,32},{32,0},{1,33},{33,1},{2,34},{34,2},{3,35},{35,3},{4,36},{36... | collective-permute-start | bytes 393224 | tf_op jit(solution)/shard_map/ppermute | solution.py:529
  (17 other events, 31.5 us)

commit v2 on v1

--- a/solution.py
+++ b/solution.py
@@ -296,13 +296,74 @@
     )(first.astype(jnp.int32).reshape(1), *ins)
 
 
+def chips_sum(pieces_ref):
+    total = pieces_ref[0].astype(F32)
+    for chip in range(1, CHIPS):
+        total += pieces_ref[chip].astype(F32)
+    return total
+
+
+def input_grad(upstream_ref, inputs_ref, total):
+    back = norm_back(inputs_ref[...].astype(F32), total, 1e-05)
+    return (upstream_ref[...].astype(F32) + back).astype(BF)
+
+
+def grad_rows(pieces, upstream, inputs):
+    def kernel(pieces_ref, upstream_ref, inputs_ref, grad_ref):
+        grad_ref[...] = input_grad(upstream_ref, inputs_ref, chips_sum(pieces_ref))
+
+    return local_call(kernel, [(inputs.shape, BF)], [pieces, upstream, inputs], "grad_rows")[0]
+
+
+def last_rows(first, gate_value, pieces, text, upstream, hidden, passed, grad):
+    def kernel(
+        first_ref,
+        gate_ref,
+        pieces_ref,
+        text_ref,
+        upstream_ref,
+        hidden_ref,
+        passed_ref,
+        grad_ref,
+        hidden_out_ref,
+        grad_out_ref,
+    ):
+        total = chips_sum(pieces_ref)
+
+        @pl.when(first_ref[0] == 1)
+        def _():
+            hidden_out_ref[...] = hidden_ref[...]
+            grad_out_ref[...] = input_grad(upstream_ref, text_ref, total)
+
+        @pl.when(first_ref[0] == 0)
+        def _():
+            term = gate_ref[0] * total
+            hidden_out_ref[...] = (passed_ref[...].astype(F32) + term).astype(BF)
+            grad_out_ref[...] = grad_ref[...]
+
+    scalar = pl.BlockSpec(memory_space=pltpu.SMEM)
+    shape = jax.ShapeDtypeStruct(text.shape, BF)
+    return pl.pallas_call(
+        kernel,
+        in_specs=[scalar, scalar] + [pl.BlockSpec()] * 6,
+        out_shape=[shape, shape],
+        compiler_params=pltpu.CompilerParams(vmem_limit_bytes=24 * 1024 * 1024),
+        name="last_rows",
+    )(
+        first.astype(jnp.int32).reshape(1),
+        gate_value.reshape(1),
+        pieces,
+        text,
+        upstream,
+        hidden,
+        passed,
+        grad,
+    )
+
+
 def token_sums(away_product, near_product, rows):
     away = away_product(rows[HALF:])
     return near_product(rows[:HALF], hop(away, TO_CORE))
-
-
-def token_totals(terms):
-    return jnp.sum(chip_exchange(terms).astype(F32), axis=0)
 
 
 def kv_product(rows, w_key, w_value, arrived=None):
@@ -474,7 +535,8 @@
 
     dmixed_second = project(*opened, w_out, True)
     mixed_first = attend(query_first, keys, values, allowed)
-    hidden_first = (text_f + gate_value * token_totals(out_sums(mixed_first))).astype(BF)
+    attended = jnp.sum(chip_exchange(out_sums(mixed_first)).astype(F32), axis=0)
+    hidden_first = (text_f + gate_value * attended).astype(BF)
 
     passed = lax.ppermute(hidden_first, "depth", [(0, 1)])
     passed_f = passed.astype(F32)
@@ -482,8 +544,7 @@
     query_second, dquery_second, dkv_second = query_back(
         *middle, w_query, dmixed_second, keys, values, allowed
     )
-    dnormed = token_totals(in_sums(dquery_second))
-    grad_second = (cotangent_f + norm_back(passed_f, dnormed, 1e-05)).astype(BF)
+    grad_second = grad_rows(chip_exchange(in_sums(dquery_second)), cotangent, passed)
     mixed_second = attend(query_second, keys, values, allowed)
 
     upstream = lax.ppermute(grad_second, "depth", [(1, 0)])
@@ -529,11 +590,16 @@
     dvision = mine + lax.ppermute(theirs, "depth", depth_swap)
     dvision = jnp.where(core == 0, dvision, dvision[::-1]).reshape(VIS // 2, vision.shape[1])
 
-    last = token_totals(last_terms)
-    grad_first = (upstream_f + norm_back(text_f, last, 1e-05)).astype(BF)
-    hidden_second = (passed_f + gate_value * last).astype(BF)
-    hidden = jnp.where(first, hidden_first, hidden_second)
-    text_grad = jnp.where(first, grad_first, grad_second)
+    hidden, text_grad = last_rows(
+        first,
+        gate_value,
+        chip_exchange(last_terms),
+        text,
+        upstream,
+        hidden_first,
+        passed,
+        grad_second,
+    )
     return (hidden[None], text_grad[None], dvision, key_grad[None], value_grad[None])
 
 

time: 295 us -> 296 us (level)
  local copies, waits for them, and re-layouts: 20.2 us -> 24.9 us
  other arithmetic: 12.3 us -> 8.15 us
  Pallas kernels: 21.3 us -> 24.8 us
    unnamed x70 -> x74, local copies, waits for them, and re-layouts: 17.2 us -> 21.8 us
    pallas_call x14 -> x15, Pallas kernels: 17.6 us -> 19.9 us  [local_call(): pl.pallas_call(kernel, in_specs=[held] * len(ins), out_specs=[held] * len...]
  transfers between devices with their start and end apart: 30 -> 30, of which waited for: 17 -> 18; matrix products, arithmetic and copies ran while one was open for 2% -> 2% of each run, Pallas kernels for 3% -> 4%
where the time goes in v2:
time: 296 us; the launch traced here: 294 us
  blocking collectives  120 us (41%)
  starting transfers between devices  68.7 us (23%)
  waiting for transfers between devices  43.2 us (15%)
  local copies, waits for them, and re-layouts  24.9 us (8%)
  Pallas kernels  24.8 us (8%)
  other arithmetic  8.15 us (3%)
  between operations  3.44 us (1%)
    all_to_all x4, blocking collectives, chip_exchange(): return lax.all_to_all(value, 'tensor', 0, 0, axis_index_groups=CHIP_GROUPS)  120 us
    ppermute x16, starting transfers between devices, hop(): return lax.ppermute(value, 'tensor', pairs)  28.9 us
    unnamed x74, local copies, waits for them, and re-layouts  21.8 us
    pallas_call x15, Pallas kernels, local_call(): pl.pallas_call(kernel, in_specs=[held] * len(ins), out_specs=[held] * len...  19.9 us
    all_to_all x3, starting transfers between devices, chip_exchange(): return lax.all_to_all(value, 'tensor', 0, 0, axis_index_groups=CHIP_GROUPS)  18 us
    all_to_all x3, waiting for transfers between devices, chip_exchange(): return lax.all_to_all(value, 'tensor', 0, 0, axis_index_groups=CHIP_GROUPS)  12.5 us
    ppermute x16, waiting for transfers between devices, hop(): return lax.ppermute(value, 'tensor', pairs)  9.93 us
    ppermute x6, starting transfers between devices, sample_hop(): return lax.ppermute(value, 'dp', pairs)  8.58 us
  transfers between devices with their start and end apart: 30, of which 18 were waited for; matrix products, arithmetic and copies ran while one was open for 2% of the time, Pallas kernels for 4%

profile of v2, /device:TPU:1, one launch (start us, length us, event | category | flops | bytes accessed | tf_op | source)
XLA Modules:
  0.0 294.2 jit_solution(13103622910543496357)
XLA Ops:
  3.4 1.4 broadcast_in_dim.16
  4.9 10.1 %all-to-all-start = ((bf16[16,4,8192]{2,1,0:T(4,128)(2,1)}), bf16[16,4,8192]{2,1,0:T(4,128)(2,1)S(1)}, u32[]{:S(2)}, u32[]{:S(2)}) async-start(bf16[16,4,8192]{2,1,0:T(4,128)(2,1)} %broadcast_in_dim.16), calls=%async_computation | async-start | bytes 2097152 | tf_op jit(solution)/shard_map/all_to_all | solution.py:47
  15.0 2.7 collective-permute-start
  17.7 2.6 collective-permute-done
  21.5 2.9 collective-permute-start.1
  24.5 2.6 collective-permute-start.4
  29.3 3.3 %collective-permute-done.4.refs_3_ = bf16[256,256]{1,0:T(8,128)(2,1)S(1)} collective-permute-done((bf16[256,256]{1,0:T(8,128)(2,1)S(1)}, bf16[256,256]{1,0:T(8,128)(2,1)S(1)}, u32[]{:S(2)}, u32[]{:S(2)}) %collective-permute-start.4) | collective-permute-done | bytes 131104 | tf_op jit(solution)/shard_map/ppermute | solution.py:497
  34.0 2.7 collective-permute-done.2.refs_1_
  37.4 3.3 %all-to-all-done.near_ref = bf16[16,4,8192]{2,1,0:T(4,128)(2,1)S(1)} async-done(((bf16[16,4,8192]{2,1,0:T(4,128)(2,1)}), bf16[16,4,8192]{2,1,0:T(4,128)(2,1)S(1)}, u32[]{:S(2)}, u32[]{:S(2)}) %all-to-all-start) | async-done | bytes 1048608 | tf_op jit(solution)/shard_map/all_to_all | solution.py:47
  40.7 2.3 collective-permute-start.5
  43.0 4.2 %all-to-all-start.1 = ((bf16[16,64,256]{2,1,0:T(8,128)(2,1)}), bf16[16,64,256]{2,1,0:T(8,128)(2,1)}, u32[]{:S(2)}, u32[]{:S(2)}) async-start(bf16[16,64,256]{2,1,0:T(8,128)(2,1)} %copy-done.10), calls=%async_computation.1 | async-start | bytes 1048576 | tf_op jit(solution)/shard_map/all_to_all | solution.py:47
  49.7 2.2 copy-done
  52.6 9.2 %all-to-all-done.1 = bf16[16,64,256]{2,1,0:T(8,128)(2,1)} async-done(((bf16[16,64,256]{2,1,0:T(8,128)(2,1)}), bf16[16,64,256]{2,1,0:T(8,128)(2,1)}, u32[]{:S(2)}, u32[]{:S(2)}) %all-to-all-start.1) | async-done | bytes 524320 | tf_op jit(solution)/shard_map/all_to_all | solution.py:47
  63.2 3.4 %collective-permute-start.8 = (bf16[64,256]{1,0:T(8,128)(2,1)S(1)}, bf16[64,256]{1,0:T(8,128)(2,1)S(1)}, u32[]{:S(2)}, u32[]{:S(2)}) collective-permute-start(bf16[64,256]{1,0:T(8,128)(2,1)S(1)} %pad_maximum_fusion.6), channel_id=1, source_target_pairs={{0,3},{1,2},{2,1},{3,0},{4,7},{5,6},{6,5},{7,4},{8,11},{9,10},{10,... | collective-permute-start | bytes 98312 | tf_op jit(solution)/shard_map/ppermute | solution.py:43
  70.9 2.2 copy-done.4
  74.1 2.5 collective-permute-done.9.arrived_ref
  77.6 28.9 %all_to_all.40 = bf16[16,4,8192]{2,1,0:T(4,128)(2,1)S(1)} all-to-all(bf16[16,4,8192]{2,1,0:T(4,128)(2,1)S(1)} %product_sum.2), channel_id=1, replica_groups={{0,2,4,6,8,10,12,14,16,18,20,22,24,26,28,30},{1,3,5,7,9,11,13,15,17,19,..., dimensions={0} | all-to-all | bytes 2097152 | tf_op jit(solution)/shard_map/all_to_all | solution.py:47
  107.0 4.5 %collective-permute-start.10 = (bf16[4,8192]{1,0:T(4,128)(2,1)S(1)}, bf16[4,8192]{1,0:T(4,128)(2,1)S(1)}, u32[]{:S(2)}, u32[]{:S(2)}) collective-permute-start(bf16[4,8192]{1,0:T(4,128)(2,1)S(1)} %fusion.6.hidden_ref), channel_id=1, source_target_pairs={{0,32},{1,33},{2,34},{3,35},{4,36},{5,37},{6,38},{7,39},{8,40},{9,... | collective-permute-start | bytes 196616 | tf_op jit(solution)/shard_map/ppermute | solution.py:541
  111.6 1.3 collective-permute-done.10.inputs_ref.passed_ref
  113.6 30.8 %all_to_all.41.near_ref = bf16[16,4,8192]{2,1,0:T(4,128)(2,1)S(1)} all-to-all(bf16[16,4,8192]{2,1,0:T(4,128)(2,1)S(1)} %broadcast_in_dim.17), channel_id=1, replica_groups={{0,2,4,6,8,10,12,14,16,18,20,22,24,26,28,30},{1,3,5,7,9,11,13,15,17,19,..., dimensions={0} | all-to-all | bytes 2097152 | tf_op jit(solution)/shard_map/all_to_all | solution.py:47
  144.4 3.0 %collective-permute-start.11 = (bf16[16,4,8192]{2,1,0:T(4,128)(2,1)S(1)}, bf16[16,4,8192]{2,1,0:T(4,128)(2,1)S(1)}, u32[]{:S(2)}, u32[]{:S(2)}) collective-permute-start(bf16[16,4,8192]{2,1,0:T(4,128)(2,1)S(1)} %all_to_all.41.near_ref), channel_id=1, source_target_pairs={{0,1},{1,0},{2,3},{3,2},{4,5},{5,4},{6,7},{7,6},{8,9},{9,8},{10,11... | collective-permute-start | bytes 3145736 | tf_op jit(solution)/shard_map/ppermute | solution.py:43
  147.4 1.5 project.3.dmixed_ref
  149.7 2.0 query_back.1
  153.0 1.4 product.3
  154.9 2.3 collective-permute-done.12.arrived_ref
  157.2 1.4 product_sum.3
  158.6 29.6 %all_to_all.42.pieces_ref = bf16[16,4,8192]{2,1,0:T(4,128)(2,1)S(1)} all-to-all(bf16[16,4,8192]{2,1,0:T(4,128)(2,1)S(1)} %product_sum.3), channel_id=1, replica_groups={{0,2,4,6,8,10,12,14,16,18,20,22,24,26,28,30},{1,3,5,7,9,11,13,15,17,19,..., dimensions={0} | all-to-all | bytes 2097152 | tf_op jit(solution)/shard_map/all_to_all | solution.py:47
  189.9 5.5 %collective-permute-done.13.upstream_ref = bf16[4,8192]{1,0:T(4,128)(2,1)S(1)} collective-permute-done((bf16[4,8192]{1,0:T(4,128)(2,1)S(1)}, bf16[4,8192]{1,0:T(4,128)(2,1)S(1)}, u32[]{:S(2)}, u32[]{:S(2)}) %collective-permute-start.13) | collective-permute-done | bytes 65568 | tf_op jit(solution)/shard_map/ppermute | solution.py:550
  196.5 30.7 %all_to_all.43.near_ref = bf16[16,4,8192]{2,1,0:T(4,128)(2,1)S(1)} all-to-all(bf16[16,4,8192]{2,1,0:T(4,128)(2,1)S(1)} %broadcast_in_dim.18), channel_id=1, replica_groups={{0,2,4,6,8,10,12,14,16,18,20,22,24,26,28,30},{1,3,5,7,9,11,13,15,17,19,..., dimensions={0} | all-to-all | bytes 2097152 | tf_op jit(solution)/shard_map/all_to_all | solution.py:47
  227.2 3.0 %collective-permute-start.14 = (bf16[16,4,8192]{2,1,0:T(4,128)(2,1)S(1)}, bf16[16,4,8192]{2,1,0:T(4,128)(2,1)}, u32[]{:S(2)}, u32[]{:S(2)}) collective-permute-start(bf16[16,4,8192]{2,1,0:T(4,128)(2,1)S(1)} %all_to_all.43.near_ref), channel_id=1, source_target_pairs={{0,1},{1,0},{2,3},{3,2},{4,5},{5,4},{6,7},{7,6},{8,9},{9,8},{10,11... | collective-permute-start | bytes 3145736 | tf_op jit(solution)/shard_map/ppermute | solution.py:43
  230.9 1.7 collective-permute-done.14.far_ref
  232.6 2.2 copy-done.6
  234.8 3.8 %dmixed_back.1 = (bf16[128,256]{1,0:T(8,128)(2,1)S(1)}, f32[256,256]{1,0:T(8,128)S(1)}) custom-call(bf16[16,4,8192]{2,1,0:T(4,128)(2,1)S(1)} %all_to_all.43.near_ref, bf16[16,4,8192]{2,1,0:T(4,128)(2,1)} %collective-permute-done.14.far_ref, bf16[256,8192]{1,0:T(8,128)(2,1)S(1)} %bitcast.32, f32[128,256]{1,0:T(8,128)S(1)} %project.2.query_ref, ...), custom_call_target="tpu_custom_call" | custom-call | tf_op jit(solution)/shard_map/dmixed_back/pallas_call | solution.py:96
  239.1 1.6 collective-permute-start.17
  240.8 1.4 chosen_product.1
  244.9 4.5 %all-to-all-start.6 = ((bf16[8,64,256]{2,1,0:T(8,128)(2,1)}), bf16[8,64,256]{2,1,0:T(8,128)(2,1)S(1)}, u32[]{:S(2)}, u32[]{:S(2)}) async-start(bf16[8,64,256]{2,1,0:T(8,128)(2,1)} %broadcast_in_dim.19), calls=%async_computation.6 | async-start | bytes 524288 | tf_op jit(solution)/shard_map/all_to_all | solution.py:51
  249.4 2.2 copy-done.3
  251.6 2.2 copy-done.7
  253.8 2.4 chosen_product_sum.1
  256.2 3.4 %all-to-all-done.6 = bf16[8,64,256]{2,1,0:T(8,128)(2,1)S(1)} async-done(((bf16[8,64,256]{2,1,0:T(8,128)(2,1)}), bf16[8,64,256]{2,1,0:T(8,128)(2,1)S(1)}, u32[]{:S(2)}, u32[]{:S(2)}) %all-to-all-start.6) | async-done | bytes 262176 | tf_op jit(solution)/shard_map/all_to_all | solution.py:51
  260.5 3.7 %all-to-all-start.7 = ((bf16[16,4,8192]{2,1,0:T(4,128)(2,1)}), bf16[16,4,8192]{2,1,0:T(4,128)(2,1)S(1)}, u32[]{:S(2)}, u32[]{:S(2)}) async-start(bf16[16,4,8192]{2,1,0:T(4,128)(2,1)} %chosen_product_sum.1), calls=%async_computation.7 | async-start | bytes 2097152 | tf_op jit(solution)/shard_map/all_to_all | solution.py:47
  265.1 1.3 collective-permute-start.22
  266.4 2.4 collective-permute-start.23
  270.1 5.8 %collective-permute-start.20 = (bf16[16,64,256]{2,1,0:T(8,128)(2,1)S(1)}, bf16[16,64,256]{2,1,0:T(8,128)(2,1)}, u32[]{:S(2)}, u32[]{:S(2)}) collective-permute-start(bf16[16,64,256]{2,1,0:T(8,128)(2,1)S(1)} %pad_maximum_fusion.near_ref), channel_id=1, source_target_pairs={{0,1},{1,0},{2,3},{3,2},{4,5},{5,4},{6,7},{7,6},{8,9},{9,8},{10,11... | collective-permute-start | bytes 1572872 | tf_op jit(solution)/shard_map/ppermute | solution.py:43
  275.9 3.5 %collective-permute-start.25 = (bf16[16,64,256]{2,1,0:T(8,128)(2,1)S(1)}, bf16[16,64,256]{2,1,0:T(8,128)(2,1)}, u32[]{:S(2)}, u32[]{:S(2)}) collective-permute-start(bf16[16,64,256]{2,1,0:T(8,128)(2,1)S(1)} %pad_maximum_fusion.1.refs_4_), channel_id=1, source_target_pairs={{0,1},{1,0},{2,3},{3,2},{4,5},{5,4},{6,7},{7,6},{8,9},{9,8},{10,11... | collective-permute-start | bytes 1572872 | tf_op jit(solution)/shard_map/ppermute | solution.py:43
  279.4 2.6 vision_back.1
  285.7 2.3 weight_back.1
  288.0 1.8 collective-permute-done.21
  (157 shorter events, 38.4 us)
Async XLA Ops:
  0.6 20.5 %copy-start.9 = (bf16[1,256,1024]{2,1,0:T(8,128)(2,1)S(1)}, bf16[1,256,1024]{2,1,0:T(8,128)(2,1)}, u32[]{:S(2)}) copy-start(bf16[1,256,1024]{2,1,0:T(8,128)(2,1)} %param.15) | copy-start | bytes 1572868
  0.6 20.5 %copy-start.8 = (bf16[1,256,1024]{2,1,0:T(8,128)(2,1)S(1)}, bf16[1,256,1024]{2,1,0:T(8,128)(2,1)}, u32[]{:S(2)}) copy-start(bf16[1,256,1024]{2,1,0:T(8,128)(2,1)} %param.14) | copy-start | bytes 1572868
  4.9 35.8 %all-to-all-start = ((bf16[16,4,8192]{2,1,0:T(4,128)(2,1)}), bf16[16,4,8192]{2,1,0:T(4,128)(2,1)S(1)}, u32[]{:S(2)}, u32[]{:S(2)}) async-start(bf16[16,4,8192]{2,1,0:T(4,128)(2,1)} %broadcast_in_dim.16), calls=%async_computation | async-start | bytes 2097152 | tf_op jit(solution)/shard_map/all_to_all | solution.py:47
  15.0 5.3 %collective-permute-start = (bf16[128,256]{1,0:T(8,128)(2,1)}, bf16[128,256]{1,0:T(8,128)(2,1)S(1)}, u32[]{:S(2)}, u32[]{:S(2)}) collective-permute-start(bf16[128,256]{1,0:T(8,128)(2,1)} %param.12), channel_id=1, source_target_pairs={{0,32},{32,0},{1,33},{33,1},{2,34},{34,2},{3,35},{35,3},{4,36},{36... | collective-permute-start | bytes 196616 | tf_op jit(solution)/shard_map/ppermute | solution.py:479
  21.5 6.6 %collective-permute-start.1 = (bf16[16,64,256]{2,1,0:T(8,128)(2,1)S(1)}, bf16[16,64,256]{2,1,0:T(8,128)(2,1)S(1)}, u32[]{:S(2)}, u32[]{:S(2)}) collective-permute-start(bf16[16,64,256]{2,1,0:T(8,128)(2,1)S(1)} %kv_product.2), channel_id=1, source_target_pairs={{0,1},{1,0},{2,3},{3,2},{4,5},{5,4},{6,7},{7,6},{8,9},{9,8},{10,11... | collective-permute-start | bytes 1572872 | tf_op jit(solution)/shard_map/ppermute | solution.py:43
  24.4 8.9 %copy-start.15 = (bf16[256,256]{1,0:T(8,128)(2,1)}, bf16[256,256]{1,0:T(8,128)(2,1)S(1)}, u32[]{:S(2)}) copy-start(bf16[256,256]{1,0:T(8,128)(2,1)S(1)} %pad_maximum_fusion.2.refs_0_) | copy-start | bytes 393220
  24.5 8.1 %collective-permute-start.4 = (bf16[256,256]{1,0:T(8,128)(2,1)S(1)}, bf16[256,256]{1,0:T(8,128)(2,1)S(1)}, u32[]{:S(2)}, u32[]{:S(2)}) collective-permute-start(bf16[256,256]{1,0:T(8,128)(2,1)S(1)} %pad_maximum_fusion.2.refs_0_), channel_id=1, source_target_pairs={{0,192},{64,0},{128,64},{192,128},{1,193},{65,1},{129,65},{193,129... | collective-permute-start | bytes 393224 | tf_op jit(solution)/shard_map/ppermute | solution.py:497
  27.0 6.3 %collective-permute-start.3 = (bf16[256,256]{1,0:T(8,128)(2,1)S(1)}, bf16[256,256]{1,0:T(8,128)(2,1)S(1)}, u32[]{:S(2)}, u32[]{:S(2)}) collective-permute-start(bf16[256,256]{1,0:T(8,128)(2,1)S(1)} %pad_maximum_fusion.2.refs_0_), channel_id=1, source_target_pairs={{0,128},{64,192},{128,0},{192,64},{1,129},{65,193},{129,1},{193,65... | collective-permute-start | bytes 393224 | tf_op jit(solution)/shard_map/ppermute | solution.py:497
  27.5 9.2 %collective-permute-start.2 = (bf16[256,256]{1,0:T(8,128)(2,1)S(1)}, bf16[256,256]{1,0:T(8,128)(2,1)S(1)}, u32[]{:S(2)}, u32[]{:S(2)}) collective-permute-start(bf16[256,256]{1,0:T(8,128)(2,1)S(1)} %pad_maximum_fusion.2.refs_0_), channel_id=1, source_target_pairs={{0,64},{64,128},{128,192},{192,0},{1,65},{65,129},{129,193},{193,1... | collective-permute-start | bytes 393224 | tf_op jit(solution)/shard_map/ppermute | solution.py:497
  29.3 37.8 %copy-start.36 = (s32[1,8,4]{1,2,0:T(4,128)S(1)}, s32[1,8,4]{1,2,0:T(4,128)}, u32[]{:S(2)}) copy-start(s32[1,8,4]{1,2,0:T(4,128)} %param.19) | copy-start | bytes 388
  40.7 9.0 %collective-permute-start.5 = (bf16[16,4,8192]{2,1,0:T(4,128)(2,1)S(1)}, bf16[16,4,8192]{2,1,0:T(4,128)(2,1)S(1)}, u32[]{:S(2)}, u32[]{:S(2)}) collective-permute-start(bf16[16,4,8192]{2,1,0:T(4,128)(2,1)S(1)} %all-to-all-done.near_ref), channel_id=1, source_target_pairs={{0,1},{1,0},{2,3},{3,2},{4,5},{5,4},{6,7},{7,6},{8,9},{9,8},{10,11... | collective-permute-start | bytes 3145736 | tf_op jit(solution)/shard_map/ppermute | solution.py:43
  43.0 18.8 %all-to-all-start.1 = ((bf16[16,64,256]{2,1,0:T(8,128)(2,1)}), bf16[16,64,256]{2,1,0:T(8,128)(2,1)}, u32[]{:S(2)}, u32[]{:S(2)}) async-start(bf16[16,64,256]{2,1,0:T(8,128)(2,1)} %copy-done.10), calls=%async_computation.1 | async-start | bytes 1048576 | tf_op jit(solution)/shard_map/all_to_all | solution.py:47
  62.9 3.7 %copy-start.34 = (f32[64,256]{1,0:T(8,128)}, f32[64,256]{1,0:T(8,128)S(1)}, u32[]{:S(2)}) copy-start(f32[64,256]{1,0:T(8,128)S(1)} %convert_reduce_fusion.1) | copy-start | bytes 196612
  63.2 5.0 %collective-permute-start.8 = (bf16[64,256]{1,0:T(8,128)(2,1)S(1)}, bf16[64,256]{1,0:T(8,128)(2,1)S(1)}, u32[]{:S(2)}, u32[]{:S(2)}) collective-permute-start(bf16[64,256]{1,0:T(8,128)(2,1)S(1)} %pad_maximum_fusion.6), channel_id=1, source_target_pairs={{0,3},{1,2},{2,1},{3,0},{4,7},{5,6},{6,5},{7,4},{8,11},{9,10},{10,... | collective-permute-start | bytes 98312 | tf_op jit(solution)/shard_map/ppermute | solution.py:43
  66.6 2.8 collective-permute-start.7
  66.6 2.8 collective-permute-start.6
  73.0 3.6 %copy-start.5 = (bf16[1,256,8192]{2,1,0:T(8,128)(2,1)S(1)}, bf16[1,256,8192]{2,1,0:T(8,128)(2,1)}, u32[]{:S(2)}) copy-start(bf16[1,256,8192]{2,1,0:T(8,128)(2,1)} %param.16) | copy-start | bytes 12582916
  73.9 2.7 collective-permute-start.9
  76.6 30.3 %copy-start.13 = (bf16[4,8192]{1,0:T(4,128)(2,1)S(1)}, bf16[4,8192]{1,0:T(4,128)(2,1)}, u32[]{:S(2)}) copy-start(bf16[4,8192]{1,0:T(4,128)(2,1)} %text_ref.1) | copy-start | bytes 196612
  107.0 6.2 %copy-start.22 = (bf16[4,8192]{1,0:T(4,128)(2,1)}, bf16[4,8192]{1,0:T(4,128)(2,1)S(1)}, u32[]{:S(2)}) copy-start(bf16[4,8192]{1,0:T(4,128)(2,1)S(1)} %fusion.6.hidden_ref) | copy-start | bytes 196612
  107.0 5.8 %collective-permute-start.10 = (bf16[4,8192]{1,0:T(4,128)(2,1)S(1)}, bf16[4,8192]{1,0:T(4,128)(2,1)S(1)}, u32[]{:S(2)}, u32[]{:S(2)}) collective-permute-start(bf16[4,8192]{1,0:T(4,128)(2,1)S(1)} %fusion.6.hidden_ref), channel_id=1, source_target_pairs={{0,32},{1,33},{2,34},{3,35},{4,36},{5,37},{6,38},{7,39},{8,40},{9,... | collective-permute-start | bytes 196616 | tf_op jit(solution)/shard_map/ppermute | solution.py:541
  112.9 75.3 %copy-start.11 = (bf16[4,8192]{1,0:T(4,128)(2,1)}, bf16[4,8192]{1,0:T(4,128)(2,1)S(1)}, u32[]{:S(2)}) copy-start(bf16[4,8192]{1,0:T(4,128)(2,1)S(1)} %collective-permute-done.10.inputs_ref.passed_ref) | copy-start | bytes 196612
  113.6 36.1 %copy-start.1 = (bf16[1,8192,256]{2,1,0:T(8,128)(2,1)S(1)}, bf16[1,8192,256]{2,1,0:T(8,128)(2,1)}, u32[]{:S(2)}) copy-start(bf16[1,8192,256]{2,1,0:T(8,128)(2,1)} %param.13) | copy-start | bytes 12582916
  144.4 5.3 %collective-permute-start.11 = (bf16[16,4,8192]{2,1,0:T(4,128)(2,1)S(1)}, bf16[16,4,8192]{2,1,0:T(4,128)(2,1)S(1)}, u32[]{:S(2)}, u32[]{:S(2)}) collective-permute-start(bf16[16,4,8192]{2,1,0:T(4,128)(2,1)S(1)} %all_to_all.41.near_ref), channel_id=1, source_target_pairs={{0,1},{1,0},{2,3},{3,2},{4,5},{5,4},{6,7},{7,6},{8,9},{9,8},{10,11... | collective-permute-start | bytes 3145736 | tf_op jit(solution)/shard_map/ppermute | solution.py:43
  154.4 2.8 collective-permute-start.12
  157.2 31.0 %copy-start.17 = (bf16[4,8192]{1,0:T(4,128)(2,1)S(1)}, bf16[4,8192]{1,0:T(4,128)(2,1)}, u32[]{:S(2)}) copy-start(bf16[4,8192]{1,0:T(4,128)(2,1)} %upstream_ref.1) | copy-start | bytes 196612
  158.6 71.6 %copy-start.33 = (f32[128,256]{1,0:T(8,128)S(1)}, f32[128,256]{1,0:T(8,128)}, u32[]{:S(2)}) copy-start(f32[128,256]{1,0:T(8,128)} %copy-done.32) | copy-start | bytes 393220
  188.5 7.9 %copy-start.18 = (bf16[4,8192]{1,0:T(4,128)(2,1)}, bf16[4,8192]{1,0:T(4,128)(2,1)S(1)}, u32[]{:S(2)}) copy-start(bf16[4,8192]{1,0:T(4,128)(2,1)S(1)} %grad_rows.1.grad_ref) | copy-start | bytes 196612
  188.6 6.8 %collective-permute-start.13 = (bf16[4,8192]{1,0:T(4,128)(2,1)S(1)}, bf16[4,8192]{1,0:T(4,128)(2,1)S(1)}, u32[]{:S(2)}, u32[]{:S(2)}) collective-permute-start(bf16[4,8192]{1,0:T(4,128)(2,1)S(1)} %grad_rows.1.grad_ref), channel_id=1, source_target_pairs={{32,0},{33,1},{34,2},{35,3},{36,4},{37,5},{38,6},{39,7},{40,8},{41... | collective-permute-start | bytes 196616 | tf_op jit(solution)/shard_map/ppermute | solution.py:550
  196.5 42.1 %copy-start.25 = (f32[256,256]{1,0:T(8,128)S(1)}, f32[256,256]{1,0:T(8,128)}, u32[]{:S(2)}) copy-start(f32[256,256]{1,0:T(8,128)} %copy-done.24) | copy-start | bytes 786436
  227.2 5.4 %collective-permute-start.14 = (bf16[16,4,8192]{2,1,0:T(4,128)(2,1)S(1)}, bf16[16,4,8192]{2,1,0:T(4,128)(2,1)}, u32[]{:S(2)}, u32[]{:S(2)}) collective-permute-start(bf16[16,4,8192]{2,1,0:T(4,128)(2,1)S(1)} %all_to_all.43.near_ref), channel_id=1, source_target_pairs={{0,1},{1,0},{2,3},{3,2},{4,5},{5,4},{6,7},{7,6},{8,9},{9,8},{10,11... | collective-permute-start | bytes 3145736 | tf_op jit(solution)/shard_map/ppermute | solution.py:43
  230.8 9.9 %copy-start.2 = (bf16[1,8192,256]{2,1,0:T(8,128)(2,1)S(1)}, bf16[1,8192,256]{2,1,0:T(8,128)(2,1)}, u32[]{:S(2)}) copy-start(bf16[1,8192,256]{2,1,0:T(8,128)(2,1)} %param.13) | copy-start | bytes 12582916
  238.6 4.3 %collective-permute-start.15 = (f32[64,256]{1,0:T(8,128)S(1)}, f32[64,256]{1,0:T(8,128)S(1)}, u32[]{:S(2)}, u32[]{:S(2)}) collective-permute-start(f32[64,256]{1,0:T(8,128)S(1)} %get-tuple-element.47), channel_id=1, source_target_pairs={{0,1},{1,0},{2,3},{3,2},{4,5},{5,4},{6,7},{7,6},{8,9},{9,8},{10,11... | collective-permute-start | bytes 196616 | tf_op jit(solution)/shard_map/ppermute | solution.py:43
  239.1 3.9 %collective-permute-start.17 = (f32[64,256]{1,0:T(8,128)S(1)}, f32[64,256]{1,0:T(8,128)S(1)}, u32[]{:S(2)}, u32[]{:S(2)}) collective-permute-start(f32[64,256]{1,0:T(8,128)S(1)} %get-tuple-element.48), channel_id=1, source_target_pairs={{0,3},{1,2},{2,1},{3,0},{4,7},{5,6},{6,5},{7,4},{8,11},{9,10},{10,... | collective-permute-start | bytes 196616 | tf_op jit(solution)/shard_map/ppermute | solution.py:43
  240.7 3.1 %collective-permute-start.16 = (f32[64,256]{1,0:T(8,128)S(1)}, f32[64,256]{1,0:T(8,128)S(1)}, u32[]{:S(2)}, u32[]{:S(2)}) collective-permute-start(f32[64,256]{1,0:T(8,128)S(1)} %get-tuple-element.49), channel_id=1, source_target_pairs={{0,2},{1,3},{2,0},{3,1},{4,6},{5,7},{6,4},{7,5},{8,10},{9,11},{10,... | collective-permute-start | bytes 196616 | tf_op jit(solution)/shard_map/ppermute | solution.py:43
  240.7 3.1 %copy-start.35 = (f32[64,256]{1,0:T(8,128)S(1)}, f32[64,256]{1,0:T(8,128)}, u32[]{:S(2)}) copy-start(f32[64,256]{1,0:T(8,128)} %copy-done.34) | copy-start | bytes 196612
  242.1 7.3 %collective-permute-start.18 = (bf16[64,8192]{1,0:T(8,128)(2,1)S(1)}, bf16[64,8192]{1,0:T(8,128)(2,1)S(1)}, u32[]{:S(2)}, u32[]{:S(2)}) collective-permute-start(bf16[64,8192]{1,0:T(8,128)(2,1)S(1)} %chosen_product.1), channel_id=1, source_target_pairs={{0,1},{1,0},{2,3},{3,2},{4,5},{5,4},{6,7},{7,6},{8,9},{9,8},{10,11... | collective-permute-start | bytes 3145736 | tf_op jit(solution)/shard_map/ppermute | solution.py:43
  244.9 14.7 %all-to-all-start.6 = ((bf16[8,64,256]{2,1,0:T(8,128)(2,1)}), bf16[8,64,256]{2,1,0:T(8,128)(2,1)S(1)}, u32[]{:S(2)}, u32[]{:S(2)}) async-start(bf16[8,64,256]{2,1,0:T(8,128)(2,1)} %broadcast_in_dim.19), calls=%async_computation.6 | async-start | bytes 524288 | tf_op jit(solution)/shard_map/all_to_all | solution.py:51
  259.6 5.2 %collective-permute-start.19 = (bf16[8,64,256]{2,1,0:T(8,128)(2,1)S(1)}, bf16[8,64,256]{2,1,0:T(8,128)(2,1)S(1)}, u32[]{:S(2)}, u32[]{:S(2)}) collective-permute-start(bf16[8,64,256]{2,1,0:T(8,128)(2,1)S(1)} %all-to-all-done.6), channel_id=1, source_target_pairs={{0,16},{1,17},{2,18},{3,19},{4,20},{5,21},{6,22},{7,23},{8,24},{9,... | collective-permute-start | bytes 786440 | tf_op jit(solution)/shard_map/ppermute | solution.py:43
  260.5 29.9 %all-to-all-start.7 = ((bf16[16,4,8192]{2,1,0:T(4,128)(2,1)}), bf16[16,4,8192]{2,1,0:T(4,128)(2,1)S(1)}, u32[]{:S(2)}, u32[]{:S(2)}) async-start(bf16[16,4,8192]{2,1,0:T(4,128)(2,1)} %chosen_product_sum.1), calls=%async_computation.7 | async-start | bytes 2097152 | tf_op jit(solution)/shard_map/all_to_all | solution.py:47
  264.9 25.6 %copy-start.12 = (bf16[4,8192]{1,0:T(4,128)(2,1)S(1)}, bf16[4,8192]{1,0:T(4,128)(2,1)}, u32[]{:S(2)}) copy-start(bf16[4,8192]{1,0:T(4,128)(2,1)} %copy-done.11) | copy-start | bytes 196612
  264.9 25.6 %copy-start.14 = (bf16[4,8192]{1,0:T(4,128)(2,1)S(1)}, bf16[4,8192]{1,0:T(4,128)(2,1)}, u32[]{:S(2)}) copy-start(bf16[4,8192]{1,0:T(4,128)(2,1)} %text_ref.1) | copy-start | bytes 196612
  265.1 10.7 %collective-permute-start.22 = (bf16[4,64,256]{2,1,0:T(8,128)(2,1)S(1)}, bf16[4,64,256]{2,1,0:T(8,128)(2,1)S(1)}, u32[]{:S(2)}, u32[]{:S(2)}) collective-permute-start(bf16[4,64,256]{2,1,0:T(8,128)(2,1)S(1)} %get-tuple-element.42), channel_id=1, source_target_pairs={{0,64},{64,128},{128,192},{192,0},{1,65},{65,129},{129,193},{193,1... | collective-permute-start | bytes 393224 | tf_op jit(solution)/shard_map/ppermute | solution.py:497
  266.4 9.4 %collective-permute-start.23 = (bf16[4,64,256]{2,1,0:T(8,128)(2,1)S(1)}, bf16[4,64,256]{2,1,0:T(8,128)(2,1)S(1)}, u32[]{:S(2)}, u32[]{:S(2)}) collective-permute-start(bf16[4,64,256]{2,1,0:T(8,128)(2,1)S(1)} %get-tuple-element.43), channel_id=1, source_target_pairs={{0,128},{64,192},{128,0},{192,64},{1,129},{65,193},{129,1},{193,65... | collective-permute-start | bytes 393224 | tf_op jit(solution)/shard_map/ppermute | solution.py:497
  268.9 7.0 %collective-permute-start.24 = (bf16[4,64,256]{2,1,0:T(8,128)(2,1)S(1)}, bf16[4,64,256]{2,1,0:T(8,128)(2,1)S(1)}, u32[]{:S(2)}, u32[]{:S(2)}) collective-permute-start(bf16[4,64,256]{2,1,0:T(8,128)(2,1)S(1)} %get-tuple-element.44), channel_id=1, source_target_pairs={{0,192},{64,0},{128,64},{192,128},{1,193},{65,1},{129,65},{193,129... | collective-permute-start | bytes 393224 | tf_op jit(solution)/shard_map/ppermute | solution.py:497
  270.1 9.3 %collective-permute-start.20 = (bf16[16,64,256]{2,1,0:T(8,128)(2,1)S(1)}, bf16[16,64,256]{2,1,0:T(8,128)(2,1)}, u32[]{:S(2)}, u32[]{:S(2)}) collective-permute-start(bf16[16,64,256]{2,1,0:T(8,128)(2,1)S(1)} %pad_maximum_fusion.near_ref), channel_id=1, source_target_pairs={{0,1},{1,0},{2,3},{3,2},{4,5},{5,4},{6,7},{7,6},{8,9},{9,8},{10,11... | collective-permute-start | bytes 1572872 | tf_op jit(solution)/shard_map/ppermute | solution.py:43
  275.9 6.2 %collective-permute-start.25 = (bf16[16,64,256]{2,1,0:T(8,128)(2,1)S(1)}, bf16[16,64,256]{2,1,0:T(8,128)(2,1)}, u32[]{:S(2)}, u32[]{:S(2)}) collective-permute-start(bf16[16,64,256]{2,1,0:T(8,128)(2,1)S(1)} %pad_maximum_fusion.1.refs_4_), channel_id=1, source_target_pairs={{0,1},{1,0},{2,3},{3,2},{4,5},{5,4},{6,7},{7,6},{8,9},{9,8},{10,11... | collective-permute-start | bytes 1572872 | tf_op jit(solution)/shard_map/ppermute | solution.py:43
  282.0 7.8 %collective-permute-start.21 = (f32[2,64,256]{2,1,0:T(8,128)S(1)}, f32[2,64,256]{2,1,0:T(8,128)S(1)}, u32[]{:S(2)}, u32[]{:S(2)}) collective-permute-start(f32[2,64,256]{2,1,0:T(8,128)S(1)} %dynamic-slice_bitcast_fusion), channel_id=1, source_target_pairs={{0,32},{32,0},{1,33},{33,1},{2,34},{34,2},{3,35},{35,3},{4,36},{36... | collective-permute-start | bytes 393224 | tf_op jit(solution)/shard_map/ppermute | solution.py:590
  (19 other events, 21.8 us)

commit v3 on v2

--- a/solution.py
+++ b/solution.py
@@ -553,12 +553,10 @@
     dquery_first, dkv_first = dmixed_back(*closing, w_out, query_first, keys, values, allowed)
 
     dkv = jnp.where(first, dkv_first, dkv_second)
-    dkv_piece = (
-        dkv[:TILE_ROWS]
-        + hop(dkv[TILE_ROWS : 2 * TILE_ROWS], TO_CORE)
-        + hop(dkv[2 * TILE_ROWS : 3 * TILE_ROWS], KV_PAIR)
-        + hop(dkv[3 * TILE_ROWS :], KV_BOTH)
-    )
+    dkv_piece = dkv[:TILE_ROWS]
+    for at, pairs in ((3, KV_BOTH), (2, KV_PAIR), (1, TO_CORE)):
+        away = dkv[at * TILE_ROWS : (at + 1) * TILE_ROWS].astype(BF)
+        dkv_piece = dkv_piece + hop(away, pairs).astype(F32)
     dkv_piece = jnp.concatenate(
         [norm_back(keys_piece, dkv_piece[:, :HD], 1e-06), dkv_piece[:, HD:]], axis=1
     ).astype(BF)

time: 296 us -> 294 us (level)
  waiting for transfers between devices: 43.2 us -> 39.3 us
    unnamed x74 -> x72, local copies, waits for them, and re-layouts: 21.8 us -> 22.7 us
  transfers between devices with their start and end apart: 30 -> 30, of which waited for: 18 -> 17; matrix products, arithmetic and copies ran while one was open for 2% -> 2% of each run, Pallas kernels for 4% -> 4%
where the time goes in v3:
time: 294 us; the launch traced here: 293 us
  blocking collectives  120 us (41%)
  starting transfers between devices  70.6 us (24%)
  waiting for transfers between devices  39.3 us (13%)
  local copies, waits for them, and re-layouts  25.8 us (9%)
  Pallas kernels  24.9 us (8%)
  other arithmetic  8.17 us (3%)
  between operations  3.37 us (1%)
    all_to_all x4, blocking collectives, chip_exchange(): return lax.all_to_all(value, 'tensor', 0, 0, axis_index_groups=CHIP_GROUPS)  120 us
    ppermute x16, starting transfers between devices, hop(): return lax.ppermute(value, 'tensor', pairs)  30.1 us
    unnamed x72, local copies, waits for them, and re-layouts  22.7 us
    pallas_call x15, Pallas kernels, local_call(): pl.pallas_call(kernel, in_specs=[held] * len(ins), out_specs=[held] * len...  19.9 us
    all_to_all x3, starting transfers between devices, chip_exchange(): return lax.all_to_all(value, 'tensor', 0, 0, axis_index_groups=CHIP_GROUPS)  18 us
    all_to_all x3, waiting for transfers between devices, chip_exchange(): return lax.all_to_all(value, 'tensor', 0, 0, axis_index_groups=CHIP_GROUPS)  12.5 us
    ppermute x6, starting transfers between devices, sample_hop(): return lax.ppermute(value, 'dp', pairs)  8.58 us
    ppermute x16, waiting for transfers between devices, hop(): return lax.ppermute(value, 'tensor', pairs)  8.13 us
  transfers between devices with their start and end apart: 30, of which 17 were waited for; matrix products, arithmetic and copies ran while one was open for 2% of the time, Pallas kernels for 4%

profile of v3, /device:TPU:1, one launch (start us, length us, event | category | flops | bytes accessed | tf_op | source)
XLA Modules:
  0.0 292.8 jit_solution(2926150375328881892)
XLA Ops:
  3.4 1.4 broadcast_in_dim.16
  4.9 10.1 %all-to-all-start = ((bf16[16,4,8192]{2,1,0:T(4,128)(2,1)}), bf16[16,4,8192]{2,1,0:T(4,128)(2,1)S(1)}, u32[]{:S(2)}, u32[]{:S(2)}) async-start(bf16[16,4,8192]{2,1,0:T(4,128)(2,1)} %broadcast_in_dim.16), calls=%async_computation | async-start | bytes 2097152 | tf_op jit(solution)/shard_map/all_to_all | solution.py:47
  15.0 2.7 collective-permute-start
  17.7 2.6 collective-permute-done
  21.5 2.9 %collective-permute-start.1 = (bf16[16,64,256]{2,1,0:T(8,128)(2,1)S(1)}, bf16[16,64,256]{2,1,0:T(8,128)(2,1)S(1)}, u32[]{:S(2)}, u32[]{:S(2)}) collective-permute-start(bf16[16,64,256]{2,1,0:T(8,128)(2,1)S(1)} %kv_product.2), channel_id=1, source_target_pairs={{0,1},{1,0},{2,3},{3,2},{4,5},{5,4},{6,7},{7,6},{8,9},{9,8},{10,11... | collective-permute-start | bytes 1572872 | tf_op jit(solution)/shard_map/ppermute | solution.py:43
  24.5 2.6 collective-permute-start.4
  29.3 3.3 %collective-permute-done.4.refs_3_ = bf16[256,256]{1,0:T(8,128)(2,1)S(1)} collective-permute-done((bf16[256,256]{1,0:T(8,128)(2,1)S(1)}, bf16[256,256]{1,0:T(8,128)(2,1)S(1)}, u32[]{:S(2)}, u32[]{:S(2)}) %collective-permute-start.4) | collective-permute-done | bytes 131104 | tf_op jit(solution)/shard_map/ppermute | solution.py:497
  34.0 2.7 collective-permute-done.2.refs_1_
  37.4 3.3 %all-to-all-done.near_ref = bf16[16,4,8192]{2,1,0:T(4,128)(2,1)S(1)} async-done(((bf16[16,4,8192]{2,1,0:T(4,128)(2,1)}), bf16[16,4,8192]{2,1,0:T(4,128)(2,1)S(1)}, u32[]{:S(2)}, u32[]{:S(2)}) %all-to-all-start) | async-done | bytes 1048608 | tf_op jit(solution)/shard_map/all_to_all | solution.py:47
  40.7 2.3 collective-permute-start.5
  43.0 4.2 %all-to-all-start.1 = ((bf16[16,64,256]{2,1,0:T(8,128)(2,1)}), bf16[16,64,256]{2,1,0:T(8,128)(2,1)}, u32[]{:S(2)}, u32[]{:S(2)}) async-start(bf16[16,64,256]{2,1,0:T(8,128)(2,1)} %copy-done.10), calls=%async_computation.1 | async-start | bytes 1048576 | tf_op jit(solution)/shard_map/all_to_all | solution.py:47
  49.7 2.2 copy-done
  52.6 9.2 %all-to-all-done.1 = bf16[16,64,256]{2,1,0:T(8,128)(2,1)} async-done(((bf16[16,64,256]{2,1,0:T(8,128)(2,1)}), bf16[16,64,256]{2,1,0:T(8,128)(2,1)}, u32[]{:S(2)}, u32[]{:S(2)}) %all-to-all-start.1) | async-done | bytes 524320 | tf_op jit(solution)/shard_map/all_to_all | solution.py:47
  63.2 3.4 %collective-permute-start.8 = (bf16[64,256]{1,0:T(8,128)(2,1)S(1)}, bf16[64,256]{1,0:T(8,128)(2,1)S(1)}, u32[]{:S(2)}, u32[]{:S(2)}) collective-permute-start(bf16[64,256]{1,0:T(8,128)(2,1)S(1)} %pad_maximum_fusion.6), channel_id=1, source_target_pairs={{0,3},{1,2},{2,1},{3,0},{4,7},{5,6},{6,5},{7,4},{8,11},{9,10},{10,... | collective-permute-start | bytes 98312 | tf_op jit(solution)/shard_map/ppermute | solution.py:43
  70.9 2.2 copy-done.4
  74.1 2.5 collective-permute-done.9.arrived_ref
  77.6 28.9 %all_to_all.40 = bf16[16,4,8192]{2,1,0:T(4,128)(2,1)S(1)} all-to-all(bf16[16,4,8192]{2,1,0:T(4,128)(2,1)S(1)} %product_sum.2), channel_id=1, replica_groups={{0,2,4,6,8,10,12,14,16,18,20,22,24,26,28,30},{1,3,5,7,9,11,13,15,17,19,..., dimensions={0} | all-to-all | bytes 2097152 | tf_op jit(solution)/shard_map/all_to_all | solution.py:47
  107.0 4.5 %collective-permute-start.10 = (bf16[4,8192]{1,0:T(4,128)(2,1)S(1)}, bf16[4,8192]{1,0:T(4,128)(2,1)S(1)}, u32[]{:S(2)}, u32[]{:S(2)}) collective-permute-start(bf16[4,8192]{1,0:T(4,128)(2,1)S(1)} %fusion.6.hidden_ref), channel_id=1, source_target_pairs={{0,32},{1,33},{2,34},{3,35},{4,36},{5,37},{6,38},{7,39},{8,40},{9,... | collective-permute-start | bytes 196616 | tf_op jit(solution)/shard_map/ppermute | solution.py:541
  113.6 30.8 %all_to_all.41.near_ref = bf16[16,4,8192]{2,1,0:T(4,128)(2,1)S(1)} all-to-all(bf16[16,4,8192]{2,1,0:T(4,128)(2,1)S(1)} %broadcast_in_dim.17), channel_id=1, replica_groups={{0,2,4,6,8,10,12,14,16,18,20,22,24,26,28,30},{1,3,5,7,9,11,13,15,17,19,..., dimensions={0} | all-to-all | bytes 2097152 | tf_op jit(solution)/shard_map/all_to_all | solution.py:47
  144.4 3.0 %collective-permute-start.11 = (bf16[16,4,8192]{2,1,0:T(4,128)(2,1)S(1)}, bf16[16,4,8192]{2,1,0:T(4,128)(2,1)S(1)}, u32[]{:S(2)}, u32[]{:S(2)}) collective-permute-start(bf16[16,4,8192]{2,1,0:T(4,128)(2,1)S(1)} %all_to_all.41.near_ref), channel_id=1, source_target_pairs={{0,1},{1,0},{2,3},{3,2},{4,5},{5,4},{6,7},{7,6},{8,9},{9,8},{10,11... | collective-permute-start | bytes 3145736 | tf_op jit(solution)/shard_map/ppermute | solution.py:43
  147.4 1.5 project.3.dmixed_ref
  149.7 2.0 query_back.1
  153.0 1.4 product.3
  154.9 2.3 collective-permute-done.12.arrived_ref
  157.1 1.4 product_sum.3
  158.5 29.4 %all_to_all.42.pieces_ref = bf16[16,4,8192]{2,1,0:T(4,128)(2,1)S(1)} all-to-all(bf16[16,4,8192]{2,1,0:T(4,128)(2,1)S(1)} %product_sum.3), channel_id=1, replica_groups={{0,2,4,6,8,10,12,14,16,18,20,22,24,26,28,30},{1,3,5,7,9,11,13,15,17,19,..., dimensions={0} | all-to-all | bytes 2097152 | tf_op jit(solution)/shard_map/all_to_all | solution.py:47
  188.4 1.3 collective-permute-start.13
  189.7 5.5 %collective-permute-done.13.upstream_ref = bf16[4,8192]{1,0:T(4,128)(2,1)S(1)} collective-permute-done((bf16[4,8192]{1,0:T(4,128)(2,1)S(1)}, bf16[4,8192]{1,0:T(4,128)(2,1)S(1)}, u32[]{:S(2)}, u32[]{:S(2)}) %collective-permute-start.13) | collective-permute-done | bytes 65568 | tf_op jit(solution)/shard_map/ppermute | solution.py:550
  195.7 30.6 %all_to_all.43.near_ref = bf16[16,4,8192]{2,1,0:T(4,128)(2,1)S(1)} all-to-all(bf16[16,4,8192]{2,1,0:T(4,128)(2,1)S(1)} %broadcast_in_dim.18), channel_id=1, replica_groups={{0,2,4,6,8,10,12,14,16,18,20,22,24,26,28,30},{1,3,5,7,9,11,13,15,17,19,..., dimensions={0} | all-to-all | bytes 2097152 | tf_op jit(solution)/shard_map/all_to_all | solution.py:47
  226.2 3.0 %collective-permute-start.14 = (bf16[16,4,8192]{2,1,0:T(4,128)(2,1)S(1)}, bf16[16,4,8192]{2,1,0:T(4,128)(2,1)}, u32[]{:S(2)}, u32[]{:S(2)}) collective-permute-start(bf16[16,4,8192]{2,1,0:T(4,128)(2,1)S(1)} %all_to_all.43.near_ref), channel_id=1, source_target_pairs={{0,1},{1,0},{2,3},{3,2},{4,5},{5,4},{6,7},{7,6},{8,9},{9,8},{10,11... | collective-permute-start | bytes 3145736 | tf_op jit(solution)/shard_map/ppermute | solution.py:43
  231.6 2.2 copy-done.6
  233.8 3.8 %dmixed_back.1 = (bf16[128,256]{1,0:T(8,128)(2,1)S(1)}, f32[256,256]{1,0:T(8,128)S(1)}) custom-call(bf16[16,4,8192]{2,1,0:T(4,128)(2,1)S(1)} %all_to_all.43.near_ref, bf16[16,4,8192]{2,1,0:T(4,128)(2,1)} %collective-permute-done.14.far_ref, bf16[256,8192]{1,0:T(8,128)(2,1)S(1)} %bitcast.32, f32[128,256]{1,0:T(8,128)S(1)} %project.2.query_ref, ...), custom_call_target="tpu_custom_call" | custom-call | tf_op jit(solution)/shard_map/dmixed_back/pallas_call | solution.py:96
  237.7 1.9 collective-permute-start.15
  239.8 1.4 chosen_product.1
  243.5 3.7 %all-to-all-start.6 = ((bf16[8,64,256]{2,1,0:T(8,128)(2,1)}), bf16[8,64,256]{2,1,0:T(8,128)(2,1)S(1)}, u32[]{:S(2)}, u32[]{:S(2)}) async-start(bf16[8,64,256]{2,1,0:T(8,128)(2,1)} %broadcast_in_dim.19), calls=%async_computation.6 | async-start | bytes 524288 | tf_op jit(solution)/shard_map/all_to_all | solution.py:51
  247.3 2.2 copy-done.3
  249.5 2.2 copy-done.7
  251.7 2.4 chosen_product_sum.1
  254.1 2.7 all-to-all-done.6
  256.8 1.5 collective-permute-start.19
  258.4 3.7 %all-to-all-start.7 = ((bf16[16,4,8192]{2,1,0:T(4,128)(2,1)}), bf16[16,4,8192]{2,1,0:T(4,128)(2,1)S(1)}, u32[]{:S(2)}, u32[]{:S(2)}) async-start(bf16[16,4,8192]{2,1,0:T(4,128)(2,1)} %chosen_product_sum.1), calls=%async_computation.7 | async-start | bytes 2097152 | tf_op jit(solution)/shard_map/all_to_all | solution.py:47
  262.4 1.3 collective-permute-start.22
  263.7 2.4 collective-permute-start.23
  267.4 6.4 %collective-permute-start.20 = (bf16[16,64,256]{2,1,0:T(8,128)(2,1)S(1)}, bf16[16,64,256]{2,1,0:T(8,128)(2,1)}, u32[]{:S(2)}, u32[]{:S(2)}) collective-permute-start(bf16[16,64,256]{2,1,0:T(8,128)(2,1)S(1)} %pad_maximum_fusion.near_ref), channel_id=1, source_target_pairs={{0,1},{1,0},{2,3},{3,2},{4,5},{5,4},{6,7},{7,6},{8,9},{9,8},{10,11... | collective-permute-start | bytes 1572872 | tf_op jit(solution)/shard_map/ppermute | solution.py:43
  273.9 3.5 %collective-permute-start.25 = (bf16[16,64,256]{2,1,0:T(8,128)(2,1)S(1)}, bf16[16,64,256]{2,1,0:T(8,128)(2,1)}, u32[]{:S(2)}, u32[]{:S(2)}) collective-permute-start(bf16[16,64,256]{2,1,0:T(8,128)(2,1)S(1)} %pad_maximum_fusion.1.refs_4_), channel_id=1, source_target_pairs={{0,1},{1,0},{2,3},{3,2},{4,5},{5,4},{6,7},{7,6},{8,9},{9,8},{10,11... | collective-permute-start | bytes 1572872 | tf_op jit(solution)/shard_map/ppermute | solution.py:43
  277.3 2.6 vision_back.1
  279.9 1.6 collective-permute-start.21
  285.1 2.3 weight_back.1
  (155 shorter events, 38.2 us)
Async XLA Ops:
  0.6 20.5 %copy-start.9 = (bf16[1,256,1024]{2,1,0:T(8,128)(2,1)S(1)}, bf16[1,256,1024]{2,1,0:T(8,128)(2,1)}, u32[]{:S(2)}) copy-start(bf16[1,256,1024]{2,1,0:T(8,128)(2,1)} %param.15) | copy-start | bytes 1572868
  0.6 20.5 %copy-start.8 = (bf16[1,256,1024]{2,1,0:T(8,128)(2,1)S(1)}, bf16[1,256,1024]{2,1,0:T(8,128)(2,1)}, u32[]{:S(2)}) copy-start(bf16[1,256,1024]{2,1,0:T(8,128)(2,1)} %param.14) | copy-start | bytes 1572868
  4.9 35.8 %all-to-all-start = ((bf16[16,4,8192]{2,1,0:T(4,128)(2,1)}), bf16[16,4,8192]{2,1,0:T(4,128)(2,1)S(1)}, u32[]{:S(2)}, u32[]{:S(2)}) async-start(bf16[16,4,8192]{2,1,0:T(4,128)(2,1)} %broadcast_in_dim.16), calls=%async_computation | async-start | bytes 2097152 | tf_op jit(solution)/shard_map/all_to_all | solution.py:47
  15.0 5.3 %collective-permute-start = (bf16[128,256]{1,0:T(8,128)(2,1)}, bf16[128,256]{1,0:T(8,128)(2,1)S(1)}, u32[]{:S(2)}, u32[]{:S(2)}) collective-permute-start(bf16[128,256]{1,0:T(8,128)(2,1)} %param.12), channel_id=1, source_target_pairs={{0,32},{32,0},{1,33},{33,1},{2,34},{34,2},{3,35},{35,3},{4,36},{36... | collective-permute-start | bytes 196616 | tf_op jit(solution)/shard_map/ppermute | solution.py:479
  21.5 6.6 %collective-permute-start.1 = (bf16[16,64,256]{2,1,0:T(8,128)(2,1)S(1)}, bf16[16,64,256]{2,1,0:T(8,128)(2,1)S(1)}, u32[]{:S(2)}, u32[]{:S(2)}) collective-permute-start(bf16[16,64,256]{2,1,0:T(8,128)(2,1)S(1)} %kv_product.2), channel_id=1, source_target_pairs={{0,1},{1,0},{2,3},{3,2},{4,5},{5,4},{6,7},{7,6},{8,9},{9,8},{10,11... | collective-permute-start | bytes 1572872 | tf_op jit(solution)/shard_map/ppermute | solution.py:43
  24.4 8.9 %copy-start.15 = (bf16[256,256]{1,0:T(8,128)(2,1)}, bf16[256,256]{1,0:T(8,128)(2,1)S(1)}, u32[]{:S(2)}) copy-start(bf16[256,256]{1,0:T(8,128)(2,1)S(1)} %pad_maximum_fusion.2.refs_0_) | copy-start | bytes 393220
  24.5 8.1 %collective-permute-start.4 = (bf16[256,256]{1,0:T(8,128)(2,1)S(1)}, bf16[256,256]{1,0:T(8,128)(2,1)S(1)}, u32[]{:S(2)}, u32[]{:S(2)}) collective-permute-start(bf16[256,256]{1,0:T(8,128)(2,1)S(1)} %pad_maximum_fusion.2.refs_0_), channel_id=1, source_target_pairs={{0,192},{64,0},{128,64},{192,128},{1,193},{65,1},{129,65},{193,129... | collective-permute-start | bytes 393224 | tf_op jit(solution)/shard_map/ppermute | solution.py:497
  27.0 6.3 %collective-permute-start.3 = (bf16[256,256]{1,0:T(8,128)(2,1)S(1)}, bf16[256,256]{1,0:T(8,128)(2,1)S(1)}, u32[]{:S(2)}, u32[]{:S(2)}) collective-permute-start(bf16[256,256]{1,0:T(8,128)(2,1)S(1)} %pad_maximum_fusion.2.refs_0_), channel_id=1, source_target_pairs={{0,128},{64,192},{128,0},{192,64},{1,129},{65,193},{129,1},{193,65... | collective-permute-start | bytes 393224 | tf_op jit(solution)/shard_map/ppermute | solution.py:497
  27.5 9.2 %collective-permute-start.2 = (bf16[256,256]{1,0:T(8,128)(2,1)S(1)}, bf16[256,256]{1,0:T(8,128)(2,1)S(1)}, u32[]{:S(2)}, u32[]{:S(2)}) collective-permute-start(bf16[256,256]{1,0:T(8,128)(2,1)S(1)} %pad_maximum_fusion.2.refs_0_), channel_id=1, source_target_pairs={{0,64},{64,128},{128,192},{192,0},{1,65},{65,129},{129,193},{193,1... | collective-permute-start | bytes 393224 | tf_op jit(solution)/shard_map/ppermute | solution.py:497
  29.3 37.8 %copy-start.35 = (s32[1,8,4]{1,2,0:T(4,128)S(1)}, s32[1,8,4]{1,2,0:T(4,128)}, u32[]{:S(2)}) copy-start(s32[1,8,4]{1,2,0:T(4,128)} %param.19) | copy-start | bytes 388
  40.7 9.0 %collective-permute-start.5 = (bf16[16,4,8192]{2,1,0:T(4,128)(2,1)S(1)}, bf16[16,4,8192]{2,1,0:T(4,128)(2,1)S(1)}, u32[]{:S(2)}, u32[]{:S(2)}) collective-permute-start(bf16[16,4,8192]{2,1,0:T(4,128)(2,1)S(1)} %all-to-all-done.near_ref), channel_id=1, source_target_pairs={{0,1},{1,0},{2,3},{3,2},{4,5},{5,4},{6,7},{7,6},{8,9},{9,8},{10,11... | collective-permute-start | bytes 3145736 | tf_op jit(solution)/shard_map/ppermute | solution.py:43
  43.0 18.8 %all-to-all-start.1 = ((bf16[16,64,256]{2,1,0:T(8,128)(2,1)}), bf16[16,64,256]{2,1,0:T(8,128)(2,1)}, u32[]{:S(2)}, u32[]{:S(2)}) async-start(bf16[16,64,256]{2,1,0:T(8,128)(2,1)} %copy-done.10), calls=%async_computation.1 | async-start | bytes 1048576 | tf_op jit(solution)/shard_map/all_to_all | solution.py:47
  49.7 2.2 copy-start
  62.9 3.7 %copy-start.33 = (f32[64,256]{1,0:T(8,128)}, f32[64,256]{1,0:T(8,128)S(1)}, u32[]{:S(2)}) copy-start(f32[64,256]{1,0:T(8,128)S(1)} %convert_reduce_fusion.1) | copy-start | bytes 196612
  63.2 5.0 %collective-permute-start.8 = (bf16[64,256]{1,0:T(8,128)(2,1)S(1)}, bf16[64,256]{1,0:T(8,128)(2,1)S(1)}, u32[]{:S(2)}, u32[]{:S(2)}) collective-permute-start(bf16[64,256]{1,0:T(8,128)(2,1)S(1)} %pad_maximum_fusion.6), channel_id=1, source_target_pairs={{0,3},{1,2},{2,1},{3,0},{4,7},{5,6},{6,5},{7,4},{8,11},{9,10},{10,... | collective-permute-start | bytes 98312 | tf_op jit(solution)/shard_map/ppermute | solution.py:43
  66.6 2.8 collective-permute-start.7
  66.6 2.8 collective-permute-start.6
  70.8 2.2 copy-start.4
  73.0 3.6 %copy-start.5 = (bf16[1,256,8192]{2,1,0:T(8,128)(2,1)S(1)}, bf16[1,256,8192]{2,1,0:T(8,128)(2,1)}, u32[]{:S(2)}) copy-start(bf16[1,256,8192]{2,1,0:T(8,128)(2,1)} %param.16) | copy-start | bytes 12582916
  73.9 2.7 collective-permute-start.9
  76.6 30.3 %copy-start.13 = (bf16[4,8192]{1,0:T(4,128)(2,1)S(1)}, bf16[4,8192]{1,0:T(4,128)(2,1)}, u32[]{:S(2)}) copy-start(bf16[4,8192]{1,0:T(4,128)(2,1)} %text_ref.1) | copy-start | bytes 196612
  107.0 5.8 %collective-permute-start.10 = (bf16[4,8192]{1,0:T(4,128)(2,1)S(1)}, bf16[4,8192]{1,0:T(4,128)(2,1)S(1)}, u32[]{:S(2)}, u32[]{:S(2)}) collective-permute-start(bf16[4,8192]{1,0:T(4,128)(2,1)S(1)} %fusion.6.hidden_ref), channel_id=1, source_target_pairs={{0,32},{1,33},{2,34},{3,35},{4,36},{5,37},{6,38},{7,39},{8,40},{9,... | collective-permute-start | bytes 196616 | tf_op jit(solution)/shard_map/ppermute | solution.py:541
  112.9 75.1 %copy-start.11 = (bf16[4,8192]{1,0:T(4,128)(2,1)}, bf16[4,8192]{1,0:T(4,128)(2,1)S(1)}, u32[]{:S(2)}) copy-start(bf16[4,8192]{1,0:T(4,128)(2,1)S(1)} %collective-permute-done.10.inputs_ref.passed_ref) | copy-start | bytes 196612
  113.6 36.1 %copy-start.1 = (bf16[1,8192,256]{2,1,0:T(8,128)(2,1)S(1)}, bf16[1,8192,256]{2,1,0:T(8,128)(2,1)}, u32[]{:S(2)}) copy-start(bf16[1,8192,256]{2,1,0:T(8,128)(2,1)} %param.13) | copy-start | bytes 12582916
  144.4 5.3 %collective-permute-start.11 = (bf16[16,4,8192]{2,1,0:T(4,128)(2,1)S(1)}, bf16[16,4,8192]{2,1,0:T(4,128)(2,1)S(1)}, u32[]{:S(2)}, u32[]{:S(2)}) collective-permute-start(bf16[16,4,8192]{2,1,0:T(4,128)(2,1)S(1)} %all_to_all.41.near_ref), channel_id=1, source_target_pairs={{0,1},{1,0},{2,3},{3,2},{4,5},{5,4},{6,7},{7,6},{8,9},{9,8},{10,11... | collective-permute-start | bytes 3145736 | tf_op jit(solution)/shard_map/ppermute | solution.py:43
  154.4 2.7 collective-permute-start.12
  157.1 30.9 %copy-start.18 = (bf16[4,8192]{1,0:T(4,128)(2,1)S(1)}, bf16[4,8192]{1,0:T(4,128)(2,1)}, u32[]{:S(2)}) copy-start(bf16[4,8192]{1,0:T(4,128)(2,1)} %upstream_ref.1) | copy-start | bytes 196612
  188.4 7.3 %copy-start.19 = (bf16[4,8192]{1,0:T(4,128)(2,1)}, bf16[4,8192]{1,0:T(4,128)(2,1)S(1)}, u32[]{:S(2)}) copy-start(bf16[4,8192]{1,0:T(4,128)(2,1)S(1)} %grad_rows.1.grad_ref) | copy-start | bytes 196612
  188.4 6.8 %collective-permute-start.13 = (bf16[4,8192]{1,0:T(4,128)(2,1)S(1)}, bf16[4,8192]{1,0:T(4,128)(2,1)S(1)}, u32[]{:S(2)}, u32[]{:S(2)}) collective-permute-start(bf16[4,8192]{1,0:T(4,128)(2,1)S(1)} %grad_rows.1.grad_ref), channel_id=1, source_target_pairs={{32,0},{33,1},{34,2},{35,3},{36,4},{37,5},{38,6},{39,7},{40,8},{41... | collective-permute-start | bytes 196616 | tf_op jit(solution)/shard_map/ppermute | solution.py:550
  195.2 34.0 %copy-start.21 = (bf16[4,8192]{1,0:T(4,128)(2,1)}, bf16[4,8192]{1,0:T(4,128)(2,1)S(1)}, u32[]{:S(2)}) copy-start(bf16[4,8192]{1,0:T(4,128)(2,1)S(1)} %collective-permute-done.13.upstream_ref) | copy-start | bytes 196612
  226.2 5.4 %collective-permute-start.14 = (bf16[16,4,8192]{2,1,0:T(4,128)(2,1)S(1)}, bf16[16,4,8192]{2,1,0:T(4,128)(2,1)}, u32[]{:S(2)}, u32[]{:S(2)}) collective-permute-start(bf16[16,4,8192]{2,1,0:T(4,128)(2,1)S(1)} %all_to_all.43.near_ref), channel_id=1, source_target_pairs={{0,1},{1,0},{2,3},{3,2},{4,5},{5,4},{6,7},{7,6},{8,9},{9,8},{10,11... | collective-permute-start | bytes 3145736 | tf_op jit(solution)/shard_map/ppermute | solution.py:43
  230.1 9.7 %copy-start.2 = (bf16[1,8192,256]{2,1,0:T(8,128)(2,1)S(1)}, bf16[1,8192,256]{2,1,0:T(8,128)(2,1)}, u32[]{:S(2)}) copy-start(bf16[1,8192,256]{2,1,0:T(8,128)(2,1)} %param.13) | copy-start | bytes 12582916
  237.7 4.3 %collective-permute-start.15 = (bf16[64,256]{1,0:T(8,128)(2,1)S(1)}, bf16[64,256]{1,0:T(8,128)(2,1)S(1)}, u32[]{:S(2)}, u32[]{:S(2)}) collective-permute-start(bf16[64,256]{1,0:T(8,128)(2,1)S(1)} %get-tuple-element.49), channel_id=1, source_target_pairs={{0,3},{1,2},{2,1},{3,0},{4,7},{5,6},{6,5},{7,4},{8,11},{9,10},{10,... | collective-permute-start | bytes 98312 | tf_op jit(solution)/shard_map/ppermute | solution.py:43
  239.6 2.5 collective-permute-start.17
  239.7 2.8 collective-permute-start.16
  239.8 2.7 copy-start.34
  241.2 6.0 %collective-permute-start.18 = (bf16[64,8192]{1,0:T(8,128)(2,1)S(1)}, bf16[64,8192]{1,0:T(8,128)(2,1)S(1)}, u32[]{:S(2)}, u32[]{:S(2)}) collective-permute-start(bf16[64,8192]{1,0:T(8,128)(2,1)S(1)} %chosen_product.1), channel_id=1, source_target_pairs={{0,1},{1,0},{2,3},{3,2},{4,5},{5,4},{6,7},{7,6},{8,9},{9,8},{10,11... | collective-permute-start | bytes 3145736 | tf_op jit(solution)/shard_map/ppermute | solution.py:43
  243.5 13.3 %all-to-all-start.6 = ((bf16[8,64,256]{2,1,0:T(8,128)(2,1)}), bf16[8,64,256]{2,1,0:T(8,128)(2,1)S(1)}, u32[]{:S(2)}, u32[]{:S(2)}) async-start(bf16[8,64,256]{2,1,0:T(8,128)(2,1)} %broadcast_in_dim.19), calls=%async_computation.6 | async-start | bytes 524288 | tf_op jit(solution)/shard_map/all_to_all | solution.py:51
  256.8 5.3 %collective-permute-start.19 = (bf16[8,64,256]{2,1,0:T(8,128)(2,1)S(1)}, bf16[8,64,256]{2,1,0:T(8,128)(2,1)S(1)}, u32[]{:S(2)}, u32[]{:S(2)}) collective-permute-start(bf16[8,64,256]{2,1,0:T(8,128)(2,1)S(1)} %all-to-all-done.6), channel_id=1, source_target_pairs={{0,16},{1,17},{2,18},{3,19},{4,20},{5,21},{6,22},{7,23},{8,24},{9,... | collective-permute-start | bytes 786440 | tf_op jit(solution)/shard_map/ppermute | solution.py:43
  258.4 30.7 %all-to-all-start.7 = ((bf16[16,4,8192]{2,1,0:T(4,128)(2,1)}), bf16[16,4,8192]{2,1,0:T(4,128)(2,1)S(1)}, u32[]{:S(2)}, u32[]{:S(2)}) async-start(bf16[16,4,8192]{2,1,0:T(4,128)(2,1)} %chosen_product_sum.1), calls=%async_computation.7 | async-start | bytes 2097152 | tf_op jit(solution)/shard_map/all_to_all | solution.py:47
  262.2 26.9 %copy-start.12 = (bf16[4,8192]{1,0:T(4,128)(2,1)S(1)}, bf16[4,8192]{1,0:T(4,128)(2,1)}, u32[]{:S(2)}) copy-start(bf16[4,8192]{1,0:T(4,128)(2,1)} %copy-done.11) | copy-start | bytes 196612
  262.2 26.9 %copy-start.14 = (bf16[4,8192]{1,0:T(4,128)(2,1)S(1)}, bf16[4,8192]{1,0:T(4,128)(2,1)}, u32[]{:S(2)}) copy-start(bf16[4,8192]{1,0:T(4,128)(2,1)} %text_ref.1) | copy-start | bytes 196612
  262.4 11.3 %collective-permute-start.22 = (bf16[4,64,256]{2,1,0:T(8,128)(2,1)S(1)}, bf16[4,64,256]{2,1,0:T(8,128)(2,1)S(1)}, u32[]{:S(2)}, u32[]{:S(2)}) collective-permute-start(bf16[4,64,256]{2,1,0:T(8,128)(2,1)S(1)} %get-tuple-element.44), channel_id=1, source_target_pairs={{0,64},{64,128},{128,192},{192,0},{1,65},{65,129},{129,193},{193,1... | collective-permute-start | bytes 393224 | tf_op jit(solution)/shard_map/ppermute | solution.py:497
  263.7 10.0 %collective-permute-start.23 = (bf16[4,64,256]{2,1,0:T(8,128)(2,1)S(1)}, bf16[4,64,256]{2,1,0:T(8,128)(2,1)S(1)}, u32[]{:S(2)}, u32[]{:S(2)}) collective-permute-start(bf16[4,64,256]{2,1,0:T(8,128)(2,1)S(1)} %get-tuple-element.45), channel_id=1, source_target_pairs={{0,128},{64,192},{128,0},{192,64},{1,129},{65,193},{129,1},{193,65... | collective-permute-start | bytes 393224 | tf_op jit(solution)/shard_map/ppermute | solution.py:497
  266.2 7.6 %collective-permute-start.24 = (bf16[4,64,256]{2,1,0:T(8,128)(2,1)S(1)}, bf16[4,64,256]{2,1,0:T(8,128)(2,1)S(1)}, u32[]{:S(2)}, u32[]{:S(2)}) collective-permute-start(bf16[4,64,256]{2,1,0:T(8,128)(2,1)S(1)} %get-tuple-element.46), channel_id=1, source_target_pairs={{0,192},{64,0},{128,64},{192,128},{1,193},{65,1},{129,65},{193,129... | collective-permute-start | bytes 393224 | tf_op jit(solution)/shard_map/ppermute | solution.py:497
  267.4 9.9 %collective-permute-start.20 = (bf16[16,64,256]{2,1,0:T(8,128)(2,1)S(1)}, bf16[16,64,256]{2,1,0:T(8,128)(2,1)}, u32[]{:S(2)}, u32[]{:S(2)}) collective-permute-start(bf16[16,64,256]{2,1,0:T(8,128)(2,1)S(1)} %pad_maximum_fusion.near_ref), channel_id=1, source_target_pairs={{0,1},{1,0},{2,3},{3,2},{4,5},{5,4},{6,7},{7,6},{8,9},{9,8},{10,11... | collective-permute-start | bytes 1572872 | tf_op jit(solution)/shard_map/ppermute | solution.py:43
  273.9 7.6 %collective-permute-start.25 = (bf16[16,64,256]{2,1,0:T(8,128)(2,1)S(1)}, bf16[16,64,256]{2,1,0:T(8,128)(2,1)}, u32[]{:S(2)}, u32[]{:S(2)}) collective-permute-start(bf16[16,64,256]{2,1,0:T(8,128)(2,1)S(1)} %pad_maximum_fusion.1.refs_4_), channel_id=1, source_target_pairs={{0,1},{1,0},{2,3},{3,2},{4,5},{5,4},{6,7},{7,6},{8,9},{9,8},{10,11... | collective-permute-start | bytes 1572872 | tf_op jit(solution)/shard_map/ppermute | solution.py:43
  279.9 8.5 %collective-permute-start.21 = (f32[2,64,256]{2,1,0:T(8,128)S(1)}, f32[2,64,256]{2,1,0:T(8,128)S(1)}, u32[]{:S(2)}, u32[]{:S(2)}) collective-permute-start(f32[2,64,256]{2,1,0:T(8,128)S(1)} %dynamic-slice_bitcast_fusion), channel_id=1, source_target_pairs={{0,32},{32,0},{1,33},{33,1},{2,34},{34,2},{3,35},{35,3},{4,36},{36... | collective-permute-start | bytes 393224 | tf_op jit(solution)/shard_map/ppermute | solution.py:588
  (18 other events, 18.4 us)
